TPU v7x, 32 devices: a whole 2x2x4 slice. The times are simulated.
32 devices in a mesh: gx: 8 (over y, x, core), gy: 4 (over z).
Axes of the slice: x: 2, y: 2, z: 4, core: 2. Of those that a mesh axis runs over, the one named last changes fastest.
Arguments:
- load_cases: float32 [16, 12, 64, 128], P('gx', 'gy')
- matrix_tiles: float32 [16, 12, 64, 320], P('gx', 'gy')
- block_cols: int32 [16, 12, 5], P('gx', 'gy'), may hold values from 1 to 18, as said below
- smoother_blocks: float32 [16, 12, 4096], P('gx', 'gy')
- near_null: float32 [16, 12, 384], P('gx', 'gy'), may hold values from -0.75 to 0.75
- coarse_map: int32 [16, 12], P('gx', 'gy'), may hold values from 0 to 31, as said below
- coarse_inverse: float32 [192, 192], P(('gx', 'gy')), as said below
Outputs:
- solution: float32 [16, 12, 64, 128], P('gx', 'gy')
- residual: float32 [16, 12, 64, 128], P('gx', 'gy')
Inputs may be any that keep to these rules, and one draw needn't show every extreme that they name: `block_cols`: each aggregate's 5 slots name the aggregate itself and its four grid neighbours, each once, in an order drawn for each aggregate, as row-major indices (row width 3 + 2) into the device's block of aggregates extended by one aggregate on every side. `coarse_map`: all aggregates of one device's block of 2 x 3 aggregates map to one coarse aggregate, and different blocks to different coarse aggregates. coarse_inverse is symmetric.
All inputs are finite; a program needn't handle non-finite values.
Results may differ from a plain program's by a relative error of at most 0.0003.
Values sent between devices are 32-bit elements; how exact they have to be, the bound alone decides.
A program may use at most 64 MiB of HBM per device.

v0:
```python
import functools

import jax
import jax.numpy as jnp
from jax import lax
from jax.experimental import pallas as pl
from jax.experimental.pallas import tpu as pltpu
from jax.sharding import PartitionSpec as P

relax_weight = 0.8
highest = lax.Precision.HIGHEST


def padded(cells, sides, width):
    for axis, dim in sides:
        count = lax.axis_size(axis)
        ends = count - 1
        head = lax.slice_in_dim(cells, 0, width, axis=dim)
        tail = lax.slice_in_dim(cells, cells.shape[dim] - width, cells.shape[dim], axis=dim)
        cells = jnp.concatenate(
            [
                lax.ppermute(tail, axis, [(i, (i + 1) % count) for i in range(ends)]),
                cells,
                lax.ppermute(head, axis, [((i + 1) % count, i) for i in range(ends)]),
            ],
            axis=dim,
        )
    return cells


def cut(v):
    hi = v.astype(jnp.bfloat16)
    return hi, (v - hi.astype(jnp.float32)).astype(jnp.bfloat16)


def stacked(v):
    hi, lo = cut(v)
    return jnp.concatenate([hi, lo, hi], axis=0)


def mm(a, b):
    return lax.dot_general(a, b, (((1,), (0,)), ((), ())), preferred_element_type=jnp.float32)


def mm_t(a, b, precision=None):
    return lax.dot_general(
        a, b, (((1,), (1,)), ((), ())), precision=precision, preferred_element_type=jnp.float32
    )


def mm3(a_cut, b):
    hi, lo = cut(b)
    return mm(a_cut[0], hi) + (mm(a_cut[0], lo) + mm(a_cut[1], hi))


def step_kernel(
    nx, ny, modes,
    b_hbm, a_hbm, cols_hbm, s_hbm, n_hbm, map_hbm, inv_hbm,
    precond_ref, image_ref, alpha_ref,
    b_ref, a_ref, cols_ref, s_ref, n_ref, map_ref, inv_ref, loaded,
    blocks, nulls, field, up, down, left, right, local, edge, smoother, info, info_all, near, coarse, coarse_all,
    sums, sums_all, halo_send, halo_recv, near_send, near_recv, col_send, col_recv,
    all_send, all_recv, sum_send, sum_recv,
):
    rows, cols, blk, cases = b_ref.shape
    count = rows * cols
    size = count * blk
    n = nx * ny
    width = info.shape[1]
    coarse_rows = n * 8
    x, y = lax.axis_index("gx"), lax.axis_index("gy")
    me = x * ny + y
    sides = (
        (x > 0, (x - 1, y)),
        (x < nx - 1, (x + 1, y)),
        (y > 0, (x, y - 1)),
        (y < ny - 1, (x, y + 1)),
    )
    halos = (up, down, left, right)

    coarse_all[...] = jnp.zeros_like(coarse_all)
    info_all[...] = jnp.zeros_like(info_all)
    told, told_all = info.at[0 : modes + 1], info_all.at[:, 0 : modes + 1]
    barrier = pltpu.get_barrier_semaphore()

    def greet(j, carry):
        peer = lax.rem(me + j, n)
        pl.semaphore_signal(
            barrier, inc=1, device_id=(peer // ny, lax.rem(peer, ny)),
            device_id_type=pl.DeviceIdType.MESH,
        )
        return carry

    lax.fori_loop(1, n, greet, 0)

    loads = [
        pltpu.make_async_copy(src, dst, loaded.at[i])
        for i, (src, dst) in enumerate(
            (
                (s_hbm, s_ref), (b_hbm, b_ref), (n_hbm, n_ref), (inv_hbm, inv_ref),
                (map_hbm, map_ref), (cols_hbm, cols_ref), (a_hbm, a_ref),
            )
        )
    ]
    for load in loads:
        load.start()

    def at_column(src, dst, k):
        copies = []
        for j in range(1, ny):
            copies.append(
                pltpu.make_async_remote_copy(
                    src_ref=src, dst_ref=dst.at[me], send_sem=col_send.at[k, j],
                    recv_sem=col_recv.at[k, ny - j],
                    device_id=(x, lax.rem(y + j, ny)), device_id_type=pl.DeviceIdType.MESH,
                )
            )
        return copies

    def pass_on(src, dst, slot, k):
        def one(j, carry):
            pltpu.make_async_remote_copy(
                src_ref=src, dst_ref=dst.at[slot], send_sem=all_send.at[k], recv_sem=all_recv.at[k],
                device_id=(lax.rem(x + j, nx), y), device_id_type=pl.DeviceIdType.MESH,
            ).start()
            return carry

        lax.fori_loop(1, nx, one, 0)

    def gather_start(src, dst, k):
        for copy in at_column(src, dst, k):
            copy.start()
        pass_on(src, dst, me, k)

    def gather_pass(src, dst, k):
        for j in list(range(1, ny, 2)) + list(range(2, ny, 2)):
            slot = x * ny + lax.rem(y + j, ny)
            pltpu.make_async_copy(src, src, col_recv.at[k, j]).wait()
            pass_on(dst.at[slot], dst, slot, k)

    def wait_many(dst, tiles, sem):
        some = dst.at[pl.ds(0, tiles)]
        pltpu.make_async_copy(some, some, sem).wait()

    def gather_end(dst, k):
        wait_many(dst, (nx - 1) * ny, all_recv.at[k])

    def gather_sent(src, dst, k):
        for copy in at_column(src, dst, k):
            copy.wait_send()
        wait_many(dst, (nx - 1) * ny, all_send.at[k])

    def halo_copies(k):
        now = field.at[k]
        out = (
            (now.at[0], down.at[k], 1),
            (now.at[rows - 1], up.at[k], 0),
            (now.at[:, 0], right.at[k], 3),
            (now.at[:, cols - 1], left.at[k], 2),
        )
        return [
            pltpu.make_async_remote_copy(
                src_ref=src, dst_ref=dst,
                send_sem=halo_send.at[k, side], recv_sem=halo_recv.at[k, lands],
                device_id=peer, device_id_type=pl.DeviceIdType.MESH,
            )
            for side, ((src, dst, lands), (_, peer)) in enumerate(zip(out, sides))
        ]

    def halo_start(k):
        for (here, _), copy in zip(sides, halo_copies(k)):
            pl.when(here)(copy.start)

    def halo_wait(k, side):
        buf = halos[side].at[k]
        pl.when(sides[side][0])(pltpu.make_async_copy(buf, buf, halo_recv.at[k, side]).wait)

    def near_copies():
        return [
            pltpu.make_async_remote_copy(
                src_ref=nulls, dst_ref=near.at[lands],
                send_sem=near_send.at[side], recv_sem=near_recv.at[lands],
                device_id=peer, device_id_type=pl.DeviceIdType.MESH,
            )
            for side, (lands, (_, peer)) in enumerate(zip((1, 0, 3, 2), sides))
        ]

    loads[0].wait()
    for i in range(rows):
        for j in range(cols):
            p = i * cols + j
            for c in range(0, blk * blk, 128):
                blocks[p, 0, c // 128 : c // 128 + 1] = s_ref[j, i : i + 1, c : c + 128]
            flat = blocks[p, 0, 0 : blk * blk // 128]
            for half in range(128 // blk):
                blocks[p, 1, pl.ds(half, blk * blk // 128, stride=128 // blk), 0:blk] = flat[
                    :, half * blk : (half + 1) * blk
                ]
    for p in range(count):
        hi, lo = cut(relax_weight * blocks[p, 1, :, 0:blk])
        smoother[p] = jnp.concatenate([hi, hi, lo], axis=1)

    def smooth(v):
        return jnp.concatenate(
            [mm(smoother[p], stacked(v[p * blk : (p + 1) * blk])) for p in range(count)], axis=0
        )

    loads[1].wait()
    b = b_ref[...].reshape(size, cases)
    first = smooth(b)
    field[0] = first.reshape(rows, cols, blk, cases)
    for side, (here, _) in enumerate(sides):

        @pl.when(jnp.logical_not(here))
        def _():
            halos[side][...] = jnp.zeros_like(halos[side])
            near[side] = jnp.zeros_like(near[side])

    for load in loads[2:5]:
        load.wait()
    nulls[...] = jnp.zeros_like(nulls)
    for i in range(rows):
        for j in range(cols):
            p = i * cols + j
            for k in range(modes):
                nulls[k : k + 1, p * blk : (p + 1) * blk] = n_ref[
                    j, i : i + 1, k * blk : (k + 1) * blk
                ]
    info[...] = jnp.zeros_like(info)
    info[0:modes, 0 : inv_ref.shape[1]] = inv_ref[...]
    info[modes : modes + 1, :] = jnp.full((1, width), map_ref[0, 0].astype(jnp.float32))

    local[...] = jnp.zeros_like(local)
    loads[5].wait()
    loads[6].wait()
    for i in range(rows):
        for j in range(cols):
            p = i * cols + j
            tiles = [a_ref[i, j, :, s * blk : (s + 1) * blk] for s in range(5)]
            names = [cols_ref[j, i, s] for s in range(5)]
            for d, (di, dj) in enumerate(((0, 0), (-1, 0), (1, 0), (0, -1), (0, 1))):
                e = (i + 1 + di) * (cols + 2) + j + 1 + dj
                tile = tiles[0] * (names[0] == e).astype(jnp.float32)
                for s in range(1, 5):
                    tile = tile + tiles[s] * (names[s] == e).astype(jnp.float32)
                hi, lo = cut(tile)
                ii, jj = i + di, j + dj
                if 0 <= ii < rows and 0 <= jj < cols:
                    q = ii * cols + jj
                    for k, part in enumerate((hi, hi, lo)):
                        at = k * size + q * blk
                        local[p * blk : (p + 1) * blk, at : at + blk] = part
                else:
                    at = (0, j, cols + j, 2 * cols + i, 2 * cols + rows + i)[d]
                    edge[at] = jnp.concatenate([hi, hi, lo], axis=1)

    pl.semaphore_wait(barrier, n - 1)
    halo_start(0)
    for (here, _), copy in zip(sides, near_copies()):
        pl.when(here)(copy.start)
    gather_start(told, told_all, 0)
    info_all[pl.ds(me, 1)] = info[...][None]

    def places():
        for j in range(cols):
            yield 0, j, j, j
        for j in range(cols):
            yield 1, j, cols + j, (rows - 1) * cols + j
        for i in range(rows):
            yield 2, i, 2 * cols + i, i * cols
        for i in range(rows):
            yield 3, i, 2 * cols + rows + i, i * cols + cols - 1

    def operate(v, k):
        inner = mm(local[...], stacked(v))
        parts = [inner[p * blk : (p + 1) * blk] for p in range(count)]
        for side in (2, 3, 0, 1):
            halo_wait(k, side)
            for at_side, at, e, p in places():
                if at_side == side:
                    parts[p] = parts[p] + mm(edge[e], stacked(halos[side][k, at]))
        return jnp.concatenate(parts, axis=0)

    own_n = nulls[...]
    own_hi, own_lo = cut(own_n)
    own_cat = jnp.concatenate([own_hi, own_hi, own_lo], axis=1)

    def restrict(v, k):
        g = mm(own_cat, stacked(v))
        coarse[k] = g
        gather_start(mine(k), theirs_all(k), 1 + k)
        coarse_all[k, pl.ds(me, 1)] = g[None]

    def mine(k):
        return coarse.at[k, 0:modes]

    def theirs_all(k):
        return coarse_all.at[k, :, 0:modes]

    r = b - operate(first, 0)
    restrict(r, 0)
    gather_pass(told, told_all, 0)

    for side, (here, _) in enumerate(sides):
        buf = near.at[side]
        pl.when(here)(pltpu.make_async_copy(buf, buf, near_recv.at[side]).wait)

    def at_rows(t, v):
        pieces = [jnp.zeros_like(v)] * 6
        pieces[t] = v
        return jnp.concatenate(pieces, axis=0)

    def across(v):
        hi, lo = cut(v)
        return jnp.concatenate([hi, lo, hi], axis=1)

    spread = mm_t(local[...], across(at_rows(0, own_n)))
    parts = [spread[p * blk : (p + 1) * blk] for p in range(count)]
    theirs = [near[side] for side in range(4)]
    facing = (
        lambda at: (rows - 1) * cols + at,
        lambda at: at,
        lambda at: at * cols + cols - 1,
        lambda at: at * cols,
    )
    for side, at, e, p in places():
        q = facing[side](at)
        block = theirs[side][:, q * blk : (q + 1) * blk]
        parts[p] = parts[p] + mm_t(edge[e], across(at_rows(1 + side, block)))
    spread = jnp.concatenate(parts, axis=0)
    eye = (
        lax.broadcasted_iota(jnp.int32, (size, size), 0)
        == lax.broadcasted_iota(jnp.int32, (size, size), 1)
    ).astype(jnp.float32).astype(jnp.bfloat16)
    prolong_cut = tuple(
        mm_t(eye, part).astype(jnp.bfloat16) for part in cut(at_rows(0, own_n))
    )

    gather_pass(mine(0), theirs_all(0), 1)
    gather_end(told_all, 0)
    inv_all = info_all[...].reshape(coarse_rows, width)
    ids = [me] + [
        jnp.clip(px, 0, nx - 1) * ny + jnp.clip(py, 0, ny - 1) for _, (px, py) in sides
    ]
    lane = lax.broadcasted_iota(jnp.int32, (8, coarse_rows), 1)
    row = lax.broadcasted_iota(jnp.int32, (8, coarse_rows), 0)
    pick = []
    for d in ids:
        tile = info_all[pl.ds(d, 1)].reshape(8, width)
        label = jnp.broadcast_to(tile[modes : modes + 1, 0:1], (8, coarse_rows))
        wanted = label * 8.0 + row.astype(jnp.float32)
        hit = jnp.where(lane.astype(jnp.float32) == wanted, 1.0, 0.0)
        pick.append(jnp.where(row < modes, hit, 0.0))
    pick.append(jnp.zeros((8, coarse_rows), jnp.float32))
    picked = lax.dot_general(
        jnp.concatenate(pick, axis=0), inv_all, (((1,), (0,)), ((), ())),
        precision=highest, preferred_element_type=jnp.float32,
    )
    lane3 = lax.broadcasted_iota(jnp.int32, (n, 8, width), 2).astype(jnp.float32)
    row3 = lax.broadcasted_iota(jnp.int32, (n, 8, width), 1)
    labels = jnp.broadcast_to(info_all[...][:, modes : modes + 1, :], (n, 8, width))
    order = jnp.where(lane3 == labels * float(modes) + row3.astype(jnp.float32), 1.0, 0.0)
    order = jnp.where(row3 < modes, order, 0.0).reshape(coarse_rows, width)
    solve = mm_t(picked, order, precision=highest)
    solve_cut = cut(solve)
    spread_cut = cut(mm3(cut(spread), solve))

    def correct(k):
        gather_end(theirs_all(k), 1 + k)
        g = coarse_all[k].reshape(coarse_rows, cases)
        return mm3(prolong_cut, mm3(solve_cut, g)), mm3(spread_cut, g)

    def relax(v, k):
        s = smooth(v)
        field[k] = s.reshape(rows, cols, blk, cases)
        halo_start(k)
        return s, v - operate(s, k)

    up_by, down_by = correct(0)
    precond = first + up_by
    r = r - down_by
    s, r = relax(r, 1)
    precond = precond + s
    s, r = relax(r, 2)
    precond = precond + s
    restrict(r, 1)
    gather_pass(mine(1), theirs_all(1), 2)
    up_by, down_by = correct(1)
    precond = precond + up_by
    r = r - down_by
    s, r = relax(r, 3)
    precond = precond + s

    image = b - r
    sums[...] = jnp.concatenate(
        [
            jnp.sum(b * precond, axis=0, keepdims=True),
            jnp.sum(precond * image, axis=0, keepdims=True),
            jnp.zeros((6, cases), jnp.float32),
        ],
        axis=0,
    )

    def share(j, carry):
        peer = lax.rem(me + j, n)
        pltpu.make_async_remote_copy(
            src_ref=sums.at[0:2], dst_ref=sums_all.at[me, 0:2], send_sem=sum_send, recv_sem=sum_recv,
            device_id=(peer // ny, lax.rem(peer, ny)), device_id_type=pl.DeviceIdType.MESH,
        ).start()
        return carry

    lax.fori_loop(1, n, share, 0)
    sums_all[pl.ds(me, 1)] = sums[...][None]
    precond_ref[...] = precond.reshape(rows, cols, blk, cases)
    image_ref[...] = image.reshape(rows, cols, blk, cases)
    pairs = sums_all.at[:, 0:2]
    wait_many(pairs, n - 1, sum_recv)
    total = jnp.sum(sums_all[:, 0:2], axis=0)
    alpha_ref[...] = total[0:1] / total[1:2]

    for k in range(4):
        for (here, _), copy in zip(sides, halo_copies(k)):
            pl.when(here)(copy.wait_send)
    for (here, _), copy in zip(sides, near_copies()):
        pl.when(here)(copy.wait_send)
    gather_sent(told, told_all, 0)
    gather_sent(mine(0), theirs_all(0), 1)
    gather_sent(mine(1), theirs_all(1), 2)
    wait_many(pairs, n - 1, sum_send)


def finish_kernel(b_ref, p_ref, i_ref, alpha_ref, sol_ref, res_ref, held, scale, sems, scale_sem):
    rows = b_ref.shape[0]
    first = pltpu.make_async_copy(alpha_ref, scale, scale_sem)
    first.start()

    def move(k, i):
        ref = (p_ref, i_ref, b_ref, sol_ref, res_ref)[k]
        ends = (ref.at[i], held.at[k, i])
        return pltpu.make_async_copy(*(ends if k < 3 else ends[::-1]), sems.at[k, i])

    for i in range(rows):
        for k in range(3):
            move(k, i).start()
    first.wait()
    alpha = scale[...].reshape(1, 1, -1)
    for i in range(rows):
        move(0, i).wait()
        held[3, i] = alpha * held[0, i]
        move(3, i).start()
        move(1, i).wait()
        move(2, i).wait()
        held[4, i] = held[2, i] - alpha * held[1, i]
        move(4, i).start()
    for i in range(rows):
        move(3, i).wait()
        move(4, i).wait()


def fused(
    nx, ny,
    load_cases, matrix_tiles, block_cols, smoother_blocks, near_null, coarse_map, coarse_inverse
):
    rows, cols, blk, cases = load_cases.shape
    count = rows * cols
    modes = near_null.shape[2] // blk
    n = nx * ny
    width = -(-coarse_inverse.shape[1] // 128) * 128
    block_cols = jnp.transpose(block_cols, (1, 0, 2))
    smoother_blocks = jnp.transpose(smoother_blocks, (1, 0, 2))
    near_null = jnp.transpose(near_null, (1, 0, 2))
    vmem = pl.BlockSpec(memory_space=pltpu.VMEM)
    hbm = pl.BlockSpec(memory_space=pltpu.HBM)
    f32, bf16 = jnp.float32, jnp.bfloat16
    shape = jax.ShapeDtypeStruct(load_cases.shape, f32)
    precond, image, alpha = pl.pallas_call(
        functools.partial(step_kernel, nx, ny, modes),
        out_shape=(shape, shape, jax.ShapeDtypeStruct((1, cases), f32)),
        in_specs=[hbm] * 7,
        out_specs=(vmem, vmem, vmem),
        scratch_shapes=[
            pltpu.VMEM(load_cases.shape, f32),
            pltpu.VMEM(matrix_tiles.shape, f32),
            pltpu.SMEM(block_cols.shape, jnp.int32),
            pltpu.VMEM(smoother_blocks.shape, f32),
            pltpu.VMEM(near_null.shape, f32),
            pltpu.SMEM(coarse_map.shape, jnp.int32),
            pltpu.VMEM(coarse_inverse.shape, f32),
            pltpu.SemaphoreType.DMA((7,)),
            pltpu.VMEM((count, 2, blk, 128), f32),
            pltpu.VMEM((8, count * blk), f32),
            pltpu.VMEM((4, rows, cols, blk, cases), f32),
            pltpu.VMEM((4, cols, blk, cases), f32),
            pltpu.VMEM((4, cols, blk, cases), f32),
            pltpu.VMEM((4, rows, blk, cases), f32),
            pltpu.VMEM((4, rows, blk, cases), f32),
            pltpu.VMEM((count * blk, 3 * count * blk), bf16),
            pltpu.VMEM((2 * (rows + cols), blk, 3 * blk), bf16),
            pltpu.VMEM((count, blk, 3 * blk), bf16),
            pltpu.VMEM((8, width), f32),
            pltpu.VMEM((n, 8, width), f32),
            pltpu.VMEM((4, 8, count * blk), f32),
            pltpu.VMEM((2, 8, cases), f32),
            pltpu.VMEM((2, n, 8, cases), f32),
            pltpu.VMEM((8, cases), f32),
            pltpu.VMEM((n, 8, cases), f32),
            pltpu.SemaphoreType.DMA((4, 4)),
            pltpu.SemaphoreType.DMA((4, 4)),
            pltpu.SemaphoreType.DMA((4,)),
            pltpu.SemaphoreType.DMA((4,)),
            pltpu.SemaphoreType.DMA((3, ny)),
            pltpu.SemaphoreType.DMA((3, ny)),
            pltpu.SemaphoreType.DMA((3,)),
            pltpu.SemaphoreType.DMA((3,)),
            pltpu.SemaphoreType.DMA,
            pltpu.SemaphoreType.DMA,
        ],
        compiler_params=pltpu.CompilerParams(
            collective_id=0, has_side_effects=True, vmem_limit_bytes=60 * 2**20
        ),
    )(
        load_cases, matrix_tiles, block_cols, smoother_blocks, near_null, coarse_map,
        coarse_inverse,
    )
    return pl.pallas_call(
        finish_kernel,
        out_shape=(shape, shape),
        in_specs=[hbm, hbm, hbm, hbm],
        out_specs=(hbm, hbm),
        scratch_shapes=[
            pltpu.VMEM((5,) + load_cases.shape, f32),
            pltpu.VMEM((1, cases), f32),
            pltpu.SemaphoreType.DMA((5, rows)),
            pltpu.SemaphoreType.DMA,
        ],
        compiler_params=pltpu.CompilerParams(vmem_limit_bytes=60 * 2**20),
    )(load_cases, precond, image, alpha)


def per_device(
    load_cases, matrix_tiles, block_cols, smoother_blocks, near_null, coarse_map, coarse_inverse
):
    agg_rows, agg_cols, block_size, case_count = load_cases.shape
    mode_count = near_null.shape[2] // block_size
    coarse_total = coarse_inverse.shape[1]
    coarse_aggs = coarse_total // mode_count
    modes = near_null.reshape(agg_rows, agg_cols, mode_count, block_size)
    inverse_blocks = smoother_blocks.reshape(agg_rows, agg_cols, block_size, block_size)

    def operate(vector_field):
        extended = padded(vector_field, (("gx", 0), ("gy", 1)), 1)
        flattened = extended.reshape(-1, block_size, case_count)
        picked = flattened[block_cols].reshape(agg_rows, agg_cols, -1, case_count)
        return jnp.einsum("ijbk,ijkr->ijbr", matrix_tiles, picked, precision=highest)

    def smooth(defect):
        return relax_weight * jnp.einsum(
            "ijab,ijbr->ijar", inverse_blocks, defect, precision=highest
        )

    def correct(defect):
        contrib = jnp.einsum("ijkb,ijbr->ijkr", modes, defect, precision=highest)
        own_part = jnp.sum(contrib, axis=(0, 1))
        my_label = coarse_map[0, 0]
        label_value = jnp.reshape(my_label.astype(jnp.float32), (1,))
        pieces, labels = (
            lax.all_gather(own_part[None], ("gx", "gy"), axis=0, tiled=True),
            lax.all_gather(label_value, ("gx", "gy"), axis=0, tiled=True),
        )
        label_ids = labels.astype(jnp.int32)
        placing = (label_ids[:, None] == jnp.arange(coarse_aggs, dtype=jnp.int32)[None, :]).astype(
            jnp.float32
        )
        ordered = jnp.einsum("dc,dkr->ckr", placing, pieces, precision=highest).reshape(
            coarse_total, case_count
        )
        own_rows = jnp.dot(coarse_inverse, ordered, precision=highest)
        solved = lax.all_gather(own_rows, ("gx", "gy"), axis=0, tiled=True)
        mine = lax.dynamic_slice_in_dim(solved, my_label * mode_count, mode_count, 0)
        coarse_back = jnp.broadcast_to(
            mine[None, None], (agg_rows, agg_cols, mode_count, case_count)
        )
        return jnp.einsum("ijkb,ijkr->ijbr", modes, coarse_back, precision=highest)

    first = smooth(load_cases)
    first = first + correct(load_cases - operate(first))
    precond = first + smooth(load_cases - operate(first))
    defect = load_cases - operate(precond)
    update = smooth(defect)
    update = update + correct(defect - operate(update))
    update = update + smooth(defect - operate(update))
    precond = precond + update
    local_aligned = jnp.sum(load_cases * precond, axis=(0, 1, 2))
    aligned = lax.psum(local_aligned, ("gx", "gy"))
    image = operate(precond)
    curved = lax.psum(jnp.sum(precond * image, axis=(0, 1, 2)), ("gx", "gy"))
    alpha = aligned / curved
    solution = alpha * precond
    residual = load_cases - alpha * image
    return (solution, residual)


def solution(mesh):
    nx, ny = mesh.shape["gx"], mesh.shape["gy"]
    step = functools.partial(fused, nx, ny) if nx * ny <= 128 else per_device
    placed = (
        P("gx", "gy", None, None),
        P("gx", "gy", None, None),
        P("gx", "gy", None),
        P("gx", "gy", None),
        P("gx", "gy", None),
        P("gx", "gy"),
        P(("gx", "gy"), None),
    )
    return jax.shard_map(
        step,
        mesh=mesh,
        in_specs=placed,
        out_specs=(P("gx", "gy", None, None), P("gx", "gy", None, None)),
        check_vma=False,
    )
```

profile of v0, /device:TPU:0, one launch (start us, length us, event | category | flops | bytes accessed | tf_op | source)
XLA Modules:
  0.0 49.1 jit_solution(7687894247168030777)
XLA Ops:
  0.6 46.6 %shard_map.86 = (f32[2,3,64,128]{3,2,1,0:T(8,128)}, f32[2,3,64,128]{3,2,1,0:T(8,128)}, f32[1,128]{1,0:T(1,128)}) custom-call(f32[2,3,64,128]{3,2,1,0:T(8,128)} %b_ref.1, f32[2,3,64,320]{3,2,1,0:T(8,128)} %a_hbm.1, s32[3,2,5]{2,1,0:T(2,128)} %bitcast.5, f32[3,2,4096]{2,1,0:T(2,128)} %bitcast.3, f32[3,2,384]{2,1,0:T(2,128)} %bitcast.4, s32[2,3]{1,0:T(2,128)} %map_hbm.1, ...), custom_call_target="tpu_custom_call" | custom-call | tf_op jit(solution)/shard_map/pallas_call | solution.py:476
  47.2 1.9 %shard_map.87 = (f32[2,3,64,128]{3,2,1,0:T(8,128)}, f32[2,3,64,128]{3,2,1,0:T(8,128)}) custom-call(f32[2,3,64,128]{3,2,1,0:T(8,128)} %b_ref.1, f32[2,3,64,128]{3,2,1,0:T(8,128)} %get-tuple-element.5.p_ref, f32[2,3,64,128]{3,2,1,0:T(8,128)} %get-tuple-element.6.i_ref, f32[1,128]{1,0:T(1,128)} %get-tuple-element.7.alpha_ref), custom_call_target="tpu_custom_call" | custom-call | tf_op jit(solution)/shard_map/pallas_call | solution.py:525
where the time goes:
time: 49.3 us; the launch traced here: 49.1 us
  Pallas kernels  48.5 us (98%)
  between operations  0.64 us (1%)
    pallas_call x1, Pallas kernels, fused(): pl.pallas_call(functools.partial(step_kernel, nx, ny, modes), out_shape=(...  46.6 us
    pallas_call x1, Pallas kernels, fused(): pl.pallas_call(finish_kernel, out_shape=(shape, shape), in_specs=[hbm, hb...  1.88 us

commit v1 on v0

--- a/solution.py
+++ b/solution.py
@@ -53,14 +53,33 @@
     return mm(a_cut[0], hi) + (mm(a_cut[0], lo) + mm(a_cut[1], hi))
 
 
+def flipped(v, mask):
+    bit = 1
+    while bit <= mask:
+        if mask & bit:
+            v = v + bit - 2 * bit * lax.rem(v // bit, 2)
+        bit *= 2
+    return v
+
+
+def far_first(nx, ny):
+    def hops(pair):
+        mx, my = pair
+        return bin(mx >> 1).count("1") + my + 0.1 * (mx & 1)
+
+    pairs = [(mx, my) for mx in range(nx) for my in range(ny) if mx or my]
+    return sorted(pairs, key=hops, reverse=True)
+
+
 def step_kernel(
     nx, ny, modes,
     b_hbm, a_hbm, cols_hbm, s_hbm, n_hbm, map_hbm, inv_hbm,
-    precond_ref, image_ref, alpha_ref,
+    precond_hbm, image_hbm, alpha_ref,
     b_ref, a_ref, cols_ref, s_ref, n_ref, map_ref, inv_ref, loaded,
     blocks, nulls, field, up, down, left, right, local, edge, smoother, info, info_all, near, coarse, coarse_all,
-    sums, sums_all, halo_send, halo_recv, near_send, near_recv, col_send, col_recv,
-    all_send, all_recv, sum_send, sum_recv,
+    sums, sums_all, spread, relaxed, relaxed_near, reach, solved, leaving,
+    halo_send, halo_recv, near_send, near_recv, relaxed_send, relaxed_recv, col_send, col_recv,
+    all_send, all_recv, direct_send, direct_recv, left_sem,
 ):
     rows, cols, blk, cases = b_ref.shape
     count = rows * cols
@@ -68,6 +87,7 @@
     n = nx * ny
     width = info.shape[1]
     coarse_rows = n * 8
+    around = spread.shape[0]
     x, y = lax.axis_index("gx"), lax.axis_index("gy")
     me = x * ny + y
     sides = (
@@ -77,21 +97,10 @@
         (y < ny - 1, (x, y + 1)),
     )
     halos = (up, down, left, right)
-
-    coarse_all[...] = jnp.zeros_like(coarse_all)
-    info_all[...] = jnp.zeros_like(info_all)
-    told, told_all = info.at[0 : modes + 1], info_all.at[:, 0 : modes + 1]
+    order_of_peers = far_first(nx, ny)
+    peers_x = [flipped(x, m) for m in range(nx)]
+    peers_y = [flipped(y, m) for m in range(ny)]
     barrier = pltpu.get_barrier_semaphore()
-
-    def greet(j, carry):
-        peer = lax.rem(me + j, n)
-        pl.semaphore_signal(
-            barrier, inc=1, device_id=(peer // ny, lax.rem(peer, ny)),
-            device_id_type=pl.DeviceIdType.MESH,
-        )
-        return carry
-
-    lax.fori_loop(1, n, greet, 0)
 
     loads = [
         pltpu.make_async_copy(src, dst, loaded.at[i])
@@ -105,50 +114,72 @@
     for load in loads:
         load.start()
 
-    def at_column(src, dst, k):
-        copies = []
-        for j in range(1, ny):
-            copies.append(
-                pltpu.make_async_remote_copy(
-                    src_ref=src, dst_ref=dst.at[me], send_sem=col_send.at[k, j],
-                    recv_sem=col_recv.at[k, ny - j],
-                    device_id=(x, lax.rem(y + j, ny)), device_id_type=pl.DeviceIdType.MESH,
-                )
+    coarse_all[...] = jnp.zeros_like(coarse_all)
+    info_all[...] = jnp.zeros_like(info_all)
+
+    for mx, my in order_of_peers:
+        pl.semaphore_signal(
+            barrier, inc=1, device_id=(peers_x[mx], peers_y[my]),
+            device_id_type=pl.DeviceIdType.MESH,
+        )
+
+    spread[...] = jnp.zeros_like(spread)
+    reach[...] = jnp.zeros_like(reach)
+    nulls[...] = jnp.zeros_like(nulls)
+    info[...] = jnp.zeros_like(info)
+    local[...] = jnp.zeros_like(local)
+    for side, (here, _) in enumerate(sides):
+
+        @pl.when(jnp.logical_not(here))
+        def _():
+            halos[side][...] = jnp.zeros_like(halos[side])
+            near[side] = jnp.zeros_like(near[side])
+            relaxed_near[side] = jnp.zeros_like(relaxed_near[side])
+
+    told, told_all = info.at[0 : modes + 1], info_all.at[:, 0 : modes + 1]
+
+    def at_column(src, dst):
+        return [
+            pltpu.make_async_remote_copy(
+                src_ref=src, dst_ref=dst.at[me], send_sem=col_send.at[j],
+                recv_sem=col_recv.at[ny - j],
+                device_id=(x, lax.rem(y + j, ny)), device_id_type=pl.DeviceIdType.MESH,
             )
-        return copies
-
-    def pass_on(src, dst, slot, k):
+            for j in range(1, ny)
+        ]
+
+    def pass_on(src, dst, slot):
         def one(j, carry):
             pltpu.make_async_remote_copy(
-                src_ref=src, dst_ref=dst.at[slot], send_sem=all_send.at[k], recv_sem=all_recv.at[k],
+                src_ref=src, dst_ref=dst.at[slot], send_sem=all_send, recv_sem=all_recv,
                 device_id=(lax.rem(x + j, nx), y), device_id_type=pl.DeviceIdType.MESH,
             ).start()
             return carry
 
         lax.fori_loop(1, nx, one, 0)
 
-    def gather_start(src, dst, k):
-        for copy in at_column(src, dst, k):
+    def told_start():
+        for copy in at_column(told, told_all):
             copy.start()
-        pass_on(src, dst, me, k)
-
-    def gather_pass(src, dst, k):
+        pass_on(told, told_all, me)
+
+    def told_pass():
         for j in list(range(1, ny, 2)) + list(range(2, ny, 2)):
             slot = x * ny + lax.rem(y + j, ny)
-            pltpu.make_async_copy(src, src, col_recv.at[k, j]).wait()
-            pass_on(dst.at[slot], dst, slot, k)
+            pltpu.make_async_copy(told, told, col_recv.at[j]).wait()
+            pass_on(told_all.at[slot], told_all, slot)
 
     def wait_many(dst, tiles, sem):
         some = dst.at[pl.ds(0, tiles)]
         pltpu.make_async_copy(some, some, sem).wait()
 
-    def gather_end(dst, k):
-        wait_many(dst, (nx - 1) * ny, all_recv.at[k])
-
-    def gather_sent(src, dst, k):
-        for copy in at_column(src, dst, k):
-            copy.wait_send()
-        wait_many(dst, (nx - 1) * ny, all_send.at[k])
+    def to_all(src, dst, k):
+        for mx, my in order_of_peers:
+            pltpu.make_async_remote_copy(
+                src_ref=src, dst_ref=dst.at[me], send_sem=direct_send.at[k],
+                recv_sem=direct_recv.at[k], device_id=(peers_x[mx], peers_y[my]),
+                device_id_type=pl.DeviceIdType.MESH,
+            ).start()
 
     def halo_copies(k):
         now = field.at[k]
@@ -175,15 +206,26 @@
         buf = halos[side].at[k]
         pl.when(sides[side][0])(pltpu.make_async_copy(buf, buf, halo_recv.at[k, side]).wait)
 
-    def near_copies():
+    def to_sides(src, dst, send, recv):
         return [
             pltpu.make_async_remote_copy(
-                src_ref=nulls, dst_ref=near.at[lands],
-                send_sem=near_send.at[side], recv_sem=near_recv.at[lands],
+                src_ref=src, dst_ref=dst.at[lands],
+                send_sem=send.at[side], recv_sem=recv.at[lands],
                 device_id=peer, device_id_type=pl.DeviceIdType.MESH,
             )
             for side, (lands, (_, peer)) in enumerate(zip((1, 0, 3, 2), sides))
         ]
+
+    def near_copies():
+        return to_sides(nulls, near, near_send, near_recv)
+
+    def relaxed_copies():
+        return to_sides(relaxed, relaxed_near, relaxed_send, relaxed_recv)
+
+    def from_sides(dst, recv):
+        for side, (here, _) in enumerate(sides):
+            buf = dst.at[side]
+            pl.when(here)(pltpu.make_async_copy(buf, buf, recv.at[side]).wait)
 
     loads[0].wait()
     for i in range(rows):
@@ -205,20 +247,16 @@
             [mm(smoother[p], stacked(v[p * blk : (p + 1) * blk])) for p in range(count)], axis=0
         )
 
+    def put(v, k):
+        field[k] = v.reshape(rows, cols, blk, cases)
+
     loads[1].wait()
     b = b_ref[...].reshape(size, cases)
     first = smooth(b)
-    field[0] = first.reshape(rows, cols, blk, cases)
-    for side, (here, _) in enumerate(sides):
-
-        @pl.when(jnp.logical_not(here))
-        def _():
-            halos[side][...] = jnp.zeros_like(halos[side])
-            near[side] = jnp.zeros_like(near[side])
+    put(first, 0)
 
     for load in loads[2:5]:
         load.wait()
-    nulls[...] = jnp.zeros_like(nulls)
     for i in range(rows):
         for j in range(cols):
             p = i * cols + j
@@ -226,11 +264,16 @@
                 nulls[k : k + 1, p * blk : (p + 1) * blk] = n_ref[
                     j, i : i + 1, k * blk : (k + 1) * blk
                 ]
-    info[...] = jnp.zeros_like(info)
     info[0:modes, 0 : inv_ref.shape[1]] = inv_ref[...]
     info[modes : modes + 1, :] = jnp.full((1, width), map_ref[0, 0].astype(jnp.float32))
 
-    local[...] = jnp.zeros_like(local)
+    pl.semaphore_wait(barrier, n - 1)
+    for (here, _), copy in zip(sides, near_copies()):
+        pl.when(here)(copy.start)
+    halo_start(0)
+    told_start()
+    info_all[pl.ds(me, 1)] = info[...][None]
+
     loads[5].wait()
     loads[6].wait()
     for i in range(rows):
@@ -254,13 +297,6 @@
                     at = (0, j, cols + j, 2 * cols + i, 2 * cols + rows + i)[d]
                     edge[at] = jnp.concatenate([hi, hi, lo], axis=1)
 
-    pl.semaphore_wait(barrier, n - 1)
-    halo_start(0)
-    for (here, _), copy in zip(sides, near_copies()):
-        pl.when(here)(copy.start)
-    gather_start(told, told_all, 0)
-    info_all[pl.ds(me, 1)] = info[...][None]
-
     def places():
         for j in range(cols):
             yield 0, j, j, j
@@ -285,113 +321,132 @@
     own_hi, own_lo = cut(own_n)
     own_cat = jnp.concatenate([own_hi, own_hi, own_lo], axis=1)
 
+    def mine(k):
+        return coarse.at[k, 0:modes]
+
+    def theirs_all(k):
+        return coarse_all.at[k, :, 0:modes]
+
     def restrict(v, k):
         g = mm(own_cat, stacked(v))
         coarse[k] = g
-        gather_start(mine(k), theirs_all(k), 1 + k)
+        to_all(mine(k), theirs_all(k), k)
         coarse_all[k, pl.ds(me, 1)] = g[None]
 
-    def mine(k):
-        return coarse.at[k, 0:modes]
-
-    def theirs_all(k):
-        return coarse_all.at[k, :, 0:modes]
-
-    r = b - operate(first, 0)
-    restrict(r, 0)
-    gather_pass(told, told_all, 0)
-
-    for side, (here, _) in enumerate(sides):
-        buf = near.at[side]
-        pl.when(here)(pltpu.make_async_copy(buf, buf, near_recv.at[side]).wait)
-
-    def at_rows(t, v):
-        pieces = [jnp.zeros_like(v)] * 6
-        pieces[t] = v
-        return jnp.concatenate(pieces, axis=0)
+    def gathered(k):
+        wait_many(theirs_all(k), n - 1, direct_recv.at[k])
+        return coarse_all[k].reshape(coarse_rows, cases)
 
     def across(v):
         hi, lo = cut(v)
         return jnp.concatenate([hi, lo, hi], axis=1)
 
-    spread = mm_t(local[...], across(at_rows(0, own_n)))
-    parts = [spread[p * blk : (p + 1) * blk] for p in range(count)]
-    theirs = [near[side] for side in range(4)]
+    r = b - operate(first, 0)
+    restrict(r, 0)
+    t = smooth(r)
+    put(t, 1)
+    halo_start(1)
+    told_pass()
+
     facing = (
         lambda at: (rows - 1) * cols + at,
         lambda at: at,
         lambda at: at * cols + cols - 1,
         lambda at: at * cols,
     )
+    spread[0:8] = mm_t(across(own_n), local[...])
+    from_sides(near, near_recv)
     for side, at, e, p in places():
         q = facing[side](at)
-        block = theirs[side][:, q * blk : (q + 1) * blk]
-        parts[p] = parts[p] + mm_t(edge[e], across(at_rows(1 + side, block)))
-    spread = jnp.concatenate(parts, axis=0)
+        spread[8 * (1 + side) : 8 * (2 + side), p * blk : (p + 1) * blk] = mm_t(
+            across(near[side, :, q * blk : (q + 1) * blk]), edge[e]
+        )
+    for p in range(count):
+        relaxed[:, p * blk : (p + 1) * blk] = mm_t(
+            across(spread[:, p * blk : (p + 1) * blk]), smoother[p]
+        )
+    for (here, _), copy in zip(sides, relaxed_copies()):
+        pl.when(here)(copy.start)
+    reach[0:around] = spread[...] - mm_t(across(relaxed[...]), local[...])
     eye = (
         lax.broadcasted_iota(jnp.int32, (size, size), 0)
         == lax.broadcasted_iota(jnp.int32, (size, size), 1)
     ).astype(jnp.float32).astype(jnp.bfloat16)
-    prolong_cut = tuple(
-        mm_t(eye, part).astype(jnp.bfloat16) for part in cut(at_rows(0, own_n))
-    )
-
-    gather_pass(mine(0), theirs_all(0), 1)
-    gather_end(told_all, 0)
-    inv_all = info_all[...].reshape(coarse_rows, width)
-    ids = [me] + [
-        jnp.clip(px, 0, nx - 1) * ny + jnp.clip(py, 0, ny - 1) for _, (px, py) in sides
-    ]
-    lane = lax.broadcasted_iota(jnp.int32, (8, coarse_rows), 1)
-    row = lax.broadcasted_iota(jnp.int32, (8, coarse_rows), 0)
-    pick = []
-    for d in ids:
-        tile = info_all[pl.ds(d, 1)].reshape(8, width)
-        label = jnp.broadcast_to(tile[modes : modes + 1, 0:1], (8, coarse_rows))
-        wanted = label * 8.0 + row.astype(jnp.float32)
-        hit = jnp.where(lane.astype(jnp.float32) == wanted, 1.0, 0.0)
-        pick.append(jnp.where(row < modes, hit, 0.0))
-    pick.append(jnp.zeros((8, coarse_rows), jnp.float32))
-    picked = lax.dot_general(
-        jnp.concatenate(pick, axis=0), inv_all, (((1,), (0,)), ((), ())),
-        precision=highest, preferred_element_type=jnp.float32,
-    )
+
+    def turned(v):
+        return tuple(mm_t(eye, part).astype(jnp.bfloat16) for part in cut(v))
+
+    gain = turned(
+        jnp.concatenate([own_n - relaxed[0:8], 0.0 - relaxed[8:around]], axis=0)
+    )
+    q1 = r - operate(t, 1)
+
+    wait_many(told_all, (nx - 1) * ny, all_recv)
+    inv_parts = cut(info_all[...].reshape(coarse_rows, width))
     lane3 = lax.broadcasted_iota(jnp.int32, (n, 8, width), 2).astype(jnp.float32)
     row3 = lax.broadcasted_iota(jnp.int32, (n, 8, width), 1)
     labels = jnp.broadcast_to(info_all[...][:, modes : modes + 1, :], (n, 8, width))
-    order = jnp.where(lane3 == labels * float(modes) + row3.astype(jnp.float32), 1.0, 0.0)
-    order = jnp.where(row3 < modes, order, 0.0).reshape(coarse_rows, width)
-    solve = mm_t(picked, order, precision=highest)
-    solve_cut = cut(solve)
-    spread_cut = cut(mm3(cut(spread), solve))
-
-    def correct(k):
-        gather_end(theirs_all(k), 1 + k)
-        g = coarse_all[k].reshape(coarse_rows, cases)
-        return mm3(prolong_cut, mm3(solve_cut, g)), mm3(spread_cut, g)
-
-    def relax(v, k):
-        s = smooth(v)
-        field[k] = s.reshape(rows, cols, blk, cases)
-        halo_start(k)
-        return s, v - operate(s, k)
-
-    up_by, down_by = correct(0)
-    precond = first + up_by
-    r = r - down_by
-    s, r = relax(r, 1)
-    precond = precond + s
-    s, r = relax(r, 2)
-    precond = precond + s
+    where3 = labels * float(modes) + row3.astype(jnp.float32)
+    order = jnp.where(lane3 == where3, 1.0, 0.0)
+    order = jnp.where(row3 < modes, order, 0.0).reshape(coarse_rows, width).astype(jnp.bfloat16)
+    lane4 = lax.broadcasted_iota(jnp.int32, (n, 8, coarse_rows), 2).astype(jnp.float32)
+    row4 = lax.broadcasted_iota(jnp.int32, (n, 8, coarse_rows), 1)
+    labels4 = jnp.broadcast_to(info_all[...][:, modes : modes + 1, 0:1], (n, 8, coarse_rows))
+    pick = jnp.where(lane4 == labels4 * 8.0 + row4.astype(jnp.float32), 1.0, 0.0)
+    pick = jnp.where(row4 < modes, pick, 0.0).reshape(coarse_rows, coarse_rows).astype(jnp.bfloat16)
+    for k, part in enumerate(inv_parts):
+        solved[k] = mm_t(mm(pick, part).astype(jnp.bfloat16), order)
+
+    def clipped(px, py):
+        return jnp.clip(px, 0, nx - 1) * ny + jnp.clip(py, 0, ny - 1)
+
+    def cross(px, py):
+        return [
+            clipped(px + dx, py + dy)
+            for dx, dy in ((0, 0), (-1, 0), (1, 0), (0, -1), (0, 1))
+        ]
+
+    ids = cross(x, y)
+    for _, (px, py) in sides:
+        ids = ids + cross(px, py)
+    lacking = jnp.zeros((reach.shape[0] - 8 * len(ids), coarse_rows), jnp.float32)
+    solve = tuple(
+        jnp.concatenate(
+            [solved[k, pl.ds(pl.multiple_of(d * 8, 8), 8)] for d in ids] + [lacking], axis=0
+        ).astype(jnp.bfloat16)
+        for k in range(2)
+    )
+
+    def mm3_cut(a_cut, b_cut):
+        return mm(a_cut[0], b_cut[0]) + (mm(a_cut[0], b_cut[1]) + mm(a_cut[1], b_cut[0]))
+
+    gain_cut = cut(mm3_cut(gain, tuple(part[0:around] for part in solve)))
+
+    from_sides(relaxed_near, relaxed_recv)
+    for side, at, e, p in places():
+        q = facing[side](at)
+        reach[around * (1 + side) : around * (2 + side), p * blk : (p + 1) * blk] = 0.0 - mm_t(
+            across(relaxed_near[side, :, q * blk : (q + 1) * blk]), edge[e]
+        )
+    loss_cut = cut(mm3_cut(turned(reach[...]), solve))
+
+    g = gathered(0)
+    r = q1 - mm3(loss_cut, g)
+    s = smooth(r)
+    put(s, 2)
+    halo_start(2)
+    precond = first + t + mm3(gain_cut, g) + s
+    r = r - operate(s, 2)
     restrict(r, 1)
-    gather_pass(mine(1), theirs_all(1), 2)
-    up_by, down_by = correct(1)
-    precond = precond + up_by
-    r = r - down_by
-    s, r = relax(r, 3)
-    precond = precond + s
-
-    image = b - r
+    t = smooth(r)
+    put(t, 3)
+    halo_start(3)
+    precond = precond + t
+    q2 = r - operate(t, 3)
+    base = b - q2
+    g = gathered(1)
+    precond = precond + mm3(gain_cut, g)
+    image = base + mm3(loss_cut, g)
     sums[...] = jnp.concatenate(
         [
             jnp.sum(b * precond, axis=0, keepdims=True),
@@ -400,33 +455,37 @@
         ],
         axis=0,
     )
-
-    def share(j, carry):
-        peer = lax.rem(me + j, n)
-        pltpu.make_async_remote_copy(
-            src_ref=sums.at[0:2], dst_ref=sums_all.at[me, 0:2], send_sem=sum_send, recv_sem=sum_recv,
-            device_id=(peer // ny, lax.rem(peer, ny)), device_id_type=pl.DeviceIdType.MESH,
-        ).start()
-        return carry
-
-    lax.fori_loop(1, n, share, 0)
+    pairs = sums_all.at[:, 0:2]
+    to_all(sums.at[0:2], pairs, 2)
     sums_all[pl.ds(me, 1)] = sums[...][None]
-    precond_ref[...] = precond.reshape(rows, cols, blk, cases)
-    image_ref[...] = image.reshape(rows, cols, blk, cases)
-    pairs = sums_all.at[:, 0:2]
-    wait_many(pairs, n - 1, sum_recv)
-    total = jnp.sum(sums_all[:, 0:2], axis=0)
-    alpha_ref[...] = total[0:1] / total[1:2]
+    leaving[0] = precond.reshape(rows, cols, blk, cases)
+    leaving[1] = image.reshape(rows, cols, blk, cases)
+    leaves = [
+        pltpu.make_async_copy(leaving.at[k], dst, left_sem.at[k])
+        for k, dst in enumerate((precond_hbm, image_hbm))
+    ]
+    for leave in leaves:
+        leave.start()
 
     for k in range(4):
         for (here, _), copy in zip(sides, halo_copies(k)):
             pl.when(here)(copy.wait_send)
     for (here, _), copy in zip(sides, near_copies()):
         pl.when(here)(copy.wait_send)
-    gather_sent(told, told_all, 0)
-    gather_sent(mine(0), theirs_all(0), 1)
-    gather_sent(mine(1), theirs_all(1), 2)
-    wait_many(pairs, n - 1, sum_send)
+    for (here, _), copy in zip(sides, relaxed_copies()):
+        pl.when(here)(copy.wait_send)
+    for copy in at_column(told, told_all):
+        copy.wait_send()
+    wait_many(told_all, (nx - 1) * ny, all_send)
+    for k in range(2):
+        wait_many(theirs_all(k), n - 1, direct_send.at[k])
+    for leave in leaves:
+        leave.wait()
+
+    wait_many(pairs, n - 1, direct_recv.at[2])
+    total = jnp.sum(sums_all[:, 0:2], axis=0)
+    alpha_ref[...] = total[0:1] / total[1:2]
+    wait_many(pairs, n - 1, direct_send.at[2])
 
 
 def finish_kernel(b_ref, p_ref, i_ref, alpha_ref, sol_ref, res_ref, held, scale, sems, scale_sem):
@@ -477,7 +536,7 @@
         functools.partial(step_kernel, nx, ny, modes),
         out_shape=(shape, shape, jax.ShapeDtypeStruct((1, cases), f32)),
         in_specs=[hbm] * 7,
-        out_specs=(vmem, vmem, vmem),
+        out_specs=(hbm, hbm, vmem),
         scratch_shapes=[
             pltpu.VMEM(load_cases.shape, f32),
             pltpu.VMEM(matrix_tiles.shape, f32),
@@ -504,16 +563,25 @@
             pltpu.VMEM((2, n, 8, cases), f32),
             pltpu.VMEM((8, cases), f32),
             pltpu.VMEM((n, 8, cases), f32),
+            pltpu.VMEM((40, count * blk), f32),
+            pltpu.VMEM((40, count * blk), f32),
+            pltpu.VMEM((4, 40, count * blk), f32),
+            pltpu.VMEM((256, count * blk), f32),
+            pltpu.VMEM((2, n * 8, n * 8), f32),
+            pltpu.VMEM((2,) + load_cases.shape, f32),
             pltpu.SemaphoreType.DMA((4, 4)),
             pltpu.SemaphoreType.DMA((4, 4)),
             pltpu.SemaphoreType.DMA((4,)),
             pltpu.SemaphoreType.DMA((4,)),
-            pltpu.SemaphoreType.DMA((3, ny)),
-            pltpu.SemaphoreType.DMA((3, ny)),
+            pltpu.SemaphoreType.DMA((4,)),
+            pltpu.SemaphoreType.DMA((4,)),
+            pltpu.SemaphoreType.DMA((ny,)),
+            pltpu.SemaphoreType.DMA((ny,)),
+            pltpu.SemaphoreType.DMA,
+            pltpu.SemaphoreType.DMA,
             pltpu.SemaphoreType.DMA((3,)),
             pltpu.SemaphoreType.DMA((3,)),
-            pltpu.SemaphoreType.DMA,
-            pltpu.SemaphoreType.DMA,
+            pltpu.SemaphoreType.DMA((2,)),
         ],
         compiler_params=pltpu.CompilerParams(
             collective_id=0, has_side_effects=True, vmem_limit_bytes=60 * 2**20
@@ -547,11 +615,22 @@
     modes = near_null.reshape(agg_rows, agg_cols, mode_count, block_size)
     inverse_blocks = smoother_blocks.reshape(agg_rows, agg_cols, block_size, block_size)
 
+    steps = ((0, 0), (-1, 0), (1, 0), (0, -1), (0, 1))
+    tiles = matrix_tiles.reshape(agg_rows, agg_cols, block_size, -1, block_size)
+    row_at = jnp.arange(agg_rows, dtype=jnp.int32)[:, None, None]
+    col_at = jnp.arange(agg_cols, dtype=jnp.int32)[None, :, None]
+    stencil = []
+    for dx, dy in steps:
+        named = block_cols == (row_at + 1 + dx) * (agg_cols + 2) + col_at + 1 + dy
+        stencil.append(jnp.sum(jnp.where(named[:, :, None, :, None], tiles, 0.0), axis=3))
+
     def operate(vector_field):
         extended = padded(vector_field, (("gx", 0), ("gy", 1)), 1)
-        flattened = extended.reshape(-1, block_size, case_count)
-        picked = flattened[block_cols].reshape(agg_rows, agg_cols, -1, case_count)
-        return jnp.einsum("ijbk,ijkr->ijbr", matrix_tiles, picked, precision=highest)
+        total = 0.0
+        for tile, (dx, dy) in zip(stencil, steps):
+            cells = extended[1 + dx : 1 + dx + agg_rows, 1 + dy : 1 + dy + agg_cols]
+            total = total + jnp.einsum("ijbk,ijkr->ijbr", tile, cells, precision=highest)
+        return total
 
     def smooth(defect):
         return relax_weight * jnp.einsum(

time: 49.3 us -> 40.3 us (0.82)
  Pallas kernels: 48.5 us -> 39.5 us
    pallas_call x1, Pallas kernels: 46.6 us -> 37.6 us  [fused(): pl.pallas_call(functools.partial(step_kernel, nx, ny, modes), out_shape=(...]
where the time goes in v1:
time: 40.3 us; the launch traced here: 40.1 us
  Pallas kernels  39.5 us (98%)
  between operations  0.64 us (2%)
    pallas_call x1, Pallas kernels, fused(): pl.pallas_call(functools.partial(step_kernel, nx, ny, modes), out_shape=(...  37.6 us
    pallas_call x1, Pallas kernels, fused(): pl.pallas_call(finish_kernel, out_shape=(shape, shape), in_specs=[hbm, hb...  1.88 us

profile of v1, /device:TPU:0, one launch (start us, length us, event | category | flops | bytes accessed | tf_op | source)
XLA Modules:
  0.0 40.1 jit_solution(5593236072895364109)
XLA Ops:
  0.6 37.6 %shard_map.86 = (f32[2,3,64,128]{3,2,1,0:T(8,128)}, f32[2,3,64,128]{3,2,1,0:T(8,128)}, f32[1,128]{1,0:T(1,128)}) custom-call(f32[2,3,64,128]{3,2,1,0:T(8,128)} %b_ref.1, f32[2,3,64,320]{3,2,1,0:T(8,128)} %a_hbm.1, s32[3,2,5]{2,1,0:T(2,128)} %bitcast.5, f32[3,2,4096]{2,1,0:T(2,128)} %bitcast.3, f32[3,2,384]{2,1,0:T(2,128)} %bitcast.4, s32[2,3]{1,0:T(2,128)} %map_hbm.1, ...), custom_call_target="tpu_custom_call" | custom-call | tf_op jit(solution)/shard_map/pallas_call | solution.py:535
  38.3 1.9 %shard_map.87 = (f32[2,3,64,128]{3,2,1,0:T(8,128)}, f32[2,3,64,128]{3,2,1,0:T(8,128)}) custom-call(f32[2,3,64,128]{3,2,1,0:T(8,128)} %b_ref.1, f32[2,3,64,128]{3,2,1,0:T(8,128)} %get-tuple-element.5.p_ref, f32[2,3,64,128]{3,2,1,0:T(8,128)} %get-tuple-element.6.i_ref, f32[1,128]{1,0:T(1,128)} %get-tuple-element.7.alpha_ref), custom_call_target="tpu_custom_call" | custom-call | tf_op jit(solution)/shard_map/pallas_call | solution.py:593

commit v2 on v1

--- a/solution.py
+++ b/solution.py
@@ -79,7 +79,7 @@
     blocks, nulls, field, up, down, left, right, local, edge, smoother, info, info_all, near, coarse, coarse_all,
     sums, sums_all, spread, relaxed, relaxed_near, reach, solved, leaving,
     halo_send, halo_recv, near_send, near_recv, relaxed_send, relaxed_recv, col_send, col_recv,
-    all_send, all_recv, direct_send, direct_recv, left_sem,
+    all_send, all_recv, direct_send, direct_recv, left_sem, entered,
 ):
     rows, cols, blk, cases = b_ref.shape
     count = rows * cols
@@ -117,7 +117,8 @@
     coarse_all[...] = jnp.zeros_like(coarse_all)
     info_all[...] = jnp.zeros_like(info_all)
 
-    for mx, my in order_of_peers:
+    lines = [pair for pair in order_of_peers if 0 in pair]
+    for mx, my in lines:
         pl.semaphore_signal(
             barrier, inc=1, device_id=(peers_x[mx], peers_y[my]),
             device_id_type=pl.DeviceIdType.MESH,
@@ -149,19 +150,11 @@
         ]
 
     def pass_on(src, dst, slot):
-        def one(j, carry):
+        for mx in range(nx - 1, 0, -1):
             pltpu.make_async_remote_copy(
                 src_ref=src, dst_ref=dst.at[slot], send_sem=all_send, recv_sem=all_recv,
-                device_id=(lax.rem(x + j, nx), y), device_id_type=pl.DeviceIdType.MESH,
+                device_id=(peers_x[mx], y), device_id_type=pl.DeviceIdType.MESH,
             ).start()
-            return carry
-
-        lax.fori_loop(1, nx, one, 0)
-
-    def told_start():
-        for copy in at_column(told, told_all):
-            copy.start()
-        pass_on(told, told_all, me)
 
     def told_pass():
         for j in list(range(1, ny, 2)) + list(range(2, ny, 2)):
@@ -267,11 +260,17 @@
     info[0:modes, 0 : inv_ref.shape[1]] = inv_ref[...]
     info[modes : modes + 1, :] = jnp.full((1, width), map_ref[0, 0].astype(jnp.float32))
 
-    pl.semaphore_wait(barrier, n - 1)
+    pl.semaphore_wait(barrier, len(lines))
     for (here, _), copy in zip(sides, near_copies()):
         pl.when(here)(copy.start)
+    for copy in at_column(told, told_all):
+        copy.start()
     halo_start(0)
-    told_start()
+    for mx in range(1, nx):
+        pl.semaphore_signal(
+            entered, inc=1, device_id=(peers_x[mx], y), device_id_type=pl.DeviceIdType.MESH
+        )
+    pass_on(told, told_all, me)
     info_all[pl.ds(me, 1)] = info[...][None]
 
     loads[5].wait()
@@ -341,13 +340,6 @@
         hi, lo = cut(v)
         return jnp.concatenate([hi, lo, hi], axis=1)
 
-    r = b - operate(first, 0)
-    restrict(r, 0)
-    t = smooth(r)
-    put(t, 1)
-    halo_start(1)
-    told_pass()
-
     facing = (
         lambda at: (rows - 1) * cols + at,
         lambda at: at,
@@ -367,6 +359,15 @@
         )
     for (here, _), copy in zip(sides, relaxed_copies()):
         pl.when(here)(copy.start)
+    told_pass()
+
+    r = b - operate(first, 0)
+    pl.semaphore_wait(entered, nx - 1)
+    restrict(r, 0)
+    t = smooth(r)
+    put(t, 1)
+    halo_start(1)
+
     reach[0:around] = spread[...] - mm_t(across(relaxed[...]), local[...])
     eye = (
         lax.broadcasted_iota(jnp.int32, (size, size), 0)
@@ -582,6 +583,7 @@
             pltpu.SemaphoreType.DMA((3,)),
             pltpu.SemaphoreType.DMA((3,)),
             pltpu.SemaphoreType.DMA((2,)),
+            pltpu.SemaphoreType.REGULAR,
         ],
         compiler_params=pltpu.CompilerParams(
             collective_id=0, has_side_effects=True, vmem_limit_bytes=60 * 2**20

time: 40.3 us -> 39.2 us (0.973)
  Pallas kernels: 39.5 us -> 38.4 us
    pallas_call x1, Pallas kernels: 37.6 us -> 36.5 us  [fused(): pl.pallas_call(functools.partial(step_kernel, nx, ny, modes), out_shape=(...]
where the time goes in v2:
time: 39.2 us; the launch traced here: 39 us
  Pallas kernels  38.4 us (98%)
  between operations  0.64 us (2%)
    pallas_call x1, Pallas kernels, fused(): pl.pallas_call(functools.partial(step_kernel, nx, ny, modes), out_shape=(...  36.5 us
    pallas_call x1, Pallas kernels, fused(): pl.pallas_call(finish_kernel, out_shape=(shape, shape), in_specs=[hbm, hb...  1.88 us

profile of v2, /device:TPU:0, one launch (start us, length us, event | category | flops | bytes accessed | tf_op | source)
XLA Modules:
  0.0 39.0 jit_solution(8991987498257541874)
XLA Ops:
  0.6 36.5 %shard_map.86 = (f32[2,3,64,128]{3,2,1,0:T(8,128)}, f32[2,3,64,128]{3,2,1,0:T(8,128)}, f32[1,128]{1,0:T(1,128)}) custom-call(f32[2,3,64,128]{3,2,1,0:T(8,128)} %b_ref.1, f32[2,3,64,320]{3,2,1,0:T(8,128)} %a_hbm.1, s32[3,2,5]{2,1,0:T(2,128)} %bitcast.5, f32[3,2,4096]{2,1,0:T(2,128)} %bitcast.3, f32[3,2,384]{2,1,0:T(2,128)} %bitcast.4, s32[2,3]{1,0:T(2,128)} %map_hbm.1, ...), custom_call_target="tpu_custom_call" | custom-call | tf_op jit(solution)/shard_map/pallas_call | solution.py:536
  37.1 1.9 %shard_map.87 = (f32[2,3,64,128]{3,2,1,0:T(8,128)}, f32[2,3,64,128]{3,2,1,0:T(8,128)}) custom-call(f32[2,3,64,128]{3,2,1,0:T(8,128)} %b_ref.1, f32[2,3,64,128]{3,2,1,0:T(8,128)} %get-tuple-element.5.p_ref, f32[2,3,64,128]{3,2,1,0:T(8,128)} %get-tuple-element.6.i_ref, f32[1,128]{1,0:T(1,128)} %get-tuple-element.7.alpha_ref), custom_call_target="tpu_custom_call" | custom-call | tf_op jit(solution)/shard_map/pallas_call | solution.py:595

commit v3 on v2

--- a/solution.py
+++ b/solution.py
@@ -380,8 +380,6 @@
     gain = turned(
         jnp.concatenate([own_n - relaxed[0:8], 0.0 - relaxed[8:around]], axis=0)
     )
-    q1 = r - operate(t, 1)
-
     wait_many(told_all, (nx - 1) * ny, all_recv)
     inv_parts = cut(info_all[...].reshape(coarse_rows, width))
     lane3 = lax.broadcasted_iota(jnp.int32, (n, 8, width), 2).astype(jnp.float32)
@@ -431,6 +429,7 @@
         )
     loss_cut = cut(mm3_cut(turned(reach[...]), solve))
 
+    q1 = r - operate(t, 1)
     g = gathered(0)
     r = q1 - mm3(loss_cut, g)
     s = smooth(r)

time: 39.2 us -> 37.3 us (0.952)
  Pallas kernels: 38.4 us -> 36.5 us
    pallas_call x1, Pallas kernels: 36.5 us -> 34.6 us  [fused(): pl.pallas_call(functools.partial(step_kernel, nx, ny, modes), out_shape=(...]
where the time goes in v3:
time: 37.3 us; the launch traced here: 37.2 us
  Pallas kernels  36.5 us (98%)
  between operations  0.64 us (2%)
    pallas_call x1, Pallas kernels, fused(): pl.pallas_call(functools.partial(step_kernel, nx, ny, modes), out_shape=(...  34.6 us
    pallas_call x1, Pallas kernels, fused(): pl.pallas_call(finish_kernel, out_shape=(shape, shape), in_specs=[hbm, hb...  1.88 us

profile of v3, /device:TPU:0, one launch (start us, length us, event | category | flops | bytes accessed | tf_op | source)
XLA Modules:
  0.0 37.2 jit_solution(17271886727649083914)
XLA Ops:
  0.6 34.6 %shard_map.86 = (f32[2,3,64,128]{3,2,1,0:T(8,128)}, f32[2,3,64,128]{3,2,1,0:T(8,128)}, f32[1,128]{1,0:T(1,128)}) custom-call(f32[2,3,64,128]{3,2,1,0:T(8,128)} %b_ref.1, f32[2,3,64,320]{3,2,1,0:T(8,128)} %a_hbm.1, s32[3,2,5]{2,1,0:T(2,128)} %bitcast.5, f32[3,2,4096]{2,1,0:T(2,128)} %bitcast.3, f32[3,2,384]{2,1,0:T(2,128)} %bitcast.4, s32[2,3]{1,0:T(2,128)} %map_hbm.1, ...), custom_call_target="tpu_custom_call" | custom-call | tf_op jit(solution)/shard_map/pallas_call | solution.py:535
  35.3 1.9 %shard_map.87 = (f32[2,3,64,128]{3,2,1,0:T(8,128)}, f32[2,3,64,128]{3,2,1,0:T(8,128)}) custom-call(f32[2,3,64,128]{3,2,1,0:T(8,128)} %b_ref.1, f32[2,3,64,128]{3,2,1,0:T(8,128)} %get-tuple-element.5.p_ref, f32[2,3,64,128]{3,2,1,0:T(8,128)} %get-tuple-element.6.i_ref, f32[1,128]{1,0:T(1,128)} %get-tuple-element.7.alpha_ref), custom_call_target="tpu_custom_call" | custom-call | tf_op jit(solution)/shard_map/pallas_call | solution.py:594

commit v4 on v3

--- a/solution.py
+++ b/solution.py
@@ -74,12 +74,12 @@
 def step_kernel(
     nx, ny, modes,
     b_hbm, a_hbm, cols_hbm, s_hbm, n_hbm, map_hbm, inv_hbm,
-    precond_hbm, image_hbm, alpha_ref,
+    solution_ref, residual_ref,
     b_ref, a_ref, cols_ref, s_ref, n_ref, map_ref, inv_ref, loaded,
     blocks, nulls, field, up, down, left, right, local, edge, smoother, info, info_all, near, coarse, coarse_all,
-    sums, sums_all, spread, relaxed, relaxed_near, reach, solved, leaving,
+    sums, sums_all, spread, relaxed, relaxed_near, reach, solved,
     halo_send, halo_recv, near_send, near_recv, relaxed_send, relaxed_recv, col_send, col_recv,
-    all_send, all_recv, direct_send, direct_recv, left_sem, entered,
+    all_send, all_recv, direct_send, direct_recv, entered,
 ):
     rows, cols, blk, cases = b_ref.shape
     count = rows * cols
@@ -458,15 +458,6 @@
     pairs = sums_all.at[:, 0:2]
     to_all(sums.at[0:2], pairs, 2)
     sums_all[pl.ds(me, 1)] = sums[...][None]
-    leaving[0] = precond.reshape(rows, cols, blk, cases)
-    leaving[1] = image.reshape(rows, cols, blk, cases)
-    leaves = [
-        pltpu.make_async_copy(leaving.at[k], dst, left_sem.at[k])
-        for k, dst in enumerate((precond_hbm, image_hbm))
-    ]
-    for leave in leaves:
-        leave.start()
-
     for k in range(4):
         for (here, _), copy in zip(sides, halo_copies(k)):
             pl.when(here)(copy.wait_send)
@@ -479,41 +470,23 @@
     wait_many(told_all, (nx - 1) * ny, all_send)
     for k in range(2):
         wait_many(theirs_all(k), n - 1, direct_send.at[k])
-    for leave in leaves:
-        leave.wait()
-
     wait_many(pairs, n - 1, direct_recv.at[2])
     total = jnp.sum(sums_all[:, 0:2], axis=0)
-    alpha_ref[...] = total[0:1] / total[1:2]
+    alpha = total[0:1] / total[1:2]
+    solution_ref[...] = (alpha * precond).reshape(rows, cols, blk, cases)
+    residual_ref[...] = (b - alpha * image).reshape(rows, cols, blk, cases)
     wait_many(pairs, n - 1, direct_send.at[2])
 
 
-def finish_kernel(b_ref, p_ref, i_ref, alpha_ref, sol_ref, res_ref, held, scale, sems, scale_sem):
-    rows = b_ref.shape[0]
-    first = pltpu.make_async_copy(alpha_ref, scale, scale_sem)
-    first.start()
-
-    def move(k, i):
-        ref = (p_ref, i_ref, b_ref, sol_ref, res_ref)[k]
-        ends = (ref.at[i], held.at[k, i])
-        return pltpu.make_async_copy(*(ends if k < 3 else ends[::-1]), sems.at[k, i])
-
-    for i in range(rows):
-        for k in range(3):
-            move(k, i).start()
-    first.wait()
-    alpha = scale[...].reshape(1, 1, -1)
-    for i in range(rows):
-        move(0, i).wait()
-        held[3, i] = alpha * held[0, i]
-        move(3, i).start()
-        move(1, i).wait()
-        move(2, i).wait()
-        held[4, i] = held[2, i] - alpha * held[1, i]
-        move(4, i).start()
-    for i in range(rows):
-        move(3, i).wait()
-        move(4, i).wait()
+def finish_kernel(s_ref, r_ref, sol_ref, res_ref, sems):
+    copies = [
+        pltpu.make_async_copy(src, dst, sems.at[k])
+        for k, (src, dst) in enumerate(((s_ref, sol_ref), (r_ref, res_ref)))
+    ]
+    for copy in copies:
+        copy.start()
+    for copy in copies:
+        copy.wait()
 
 
 def fused(
@@ -532,11 +505,12 @@
     hbm = pl.BlockSpec(memory_space=pltpu.HBM)
     f32, bf16 = jnp.float32, jnp.bfloat16
     shape = jax.ShapeDtypeStruct(load_cases.shape, f32)
-    precond, image, alpha = pl.pallas_call(
+    held = pltpu.VMEM(load_cases.shape, f32)
+    solved, residual = pl.pallas_call(
         functools.partial(step_kernel, nx, ny, modes),
-        out_shape=(shape, shape, jax.ShapeDtypeStruct((1, cases), f32)),
+        out_shape=(held, held),
         in_specs=[hbm] * 7,
-        out_specs=(hbm, hbm, vmem),
+        out_specs=(vmem, vmem),
         scratch_shapes=[
             pltpu.VMEM(load_cases.shape, f32),
             pltpu.VMEM(matrix_tiles.shape, f32),
@@ -568,7 +542,6 @@
             pltpu.VMEM((4, 40, count * blk), f32),
             pltpu.VMEM((256, count * blk), f32),
             pltpu.VMEM((2, n * 8, n * 8), f32),
-            pltpu.VMEM((2,) + load_cases.shape, f32),
             pltpu.SemaphoreType.DMA((4, 4)),
             pltpu.SemaphoreType.DMA((4, 4)),
             pltpu.SemaphoreType.DMA((4,)),
@@ -581,29 +554,30 @@
             pltpu.SemaphoreType.DMA,
             pltpu.SemaphoreType.DMA((3,)),
             pltpu.SemaphoreType.DMA((3,)),
-            pltpu.SemaphoreType.DMA((2,)),
             pltpu.SemaphoreType.REGULAR,
         ],
         compiler_params=pltpu.CompilerParams(
-            collective_id=0, has_side_effects=True, vmem_limit_bytes=60 * 2**20
+            collective_id=0, has_side_effects=True, vmem_limit_bytes=32 * 2**20
         ),
     )(
-        load_cases, matrix_tiles, block_cols, smoother_blocks, near_null, coarse_map,
-        coarse_inverse,
+        *(
+            pltpu.with_memory_space_constraint(v, pltpu.HBM)
+            for v in (
+                load_cases, matrix_tiles, block_cols, smoother_blocks, near_null, coarse_map,
+                coarse_inverse,
+            )
+        )
     )
     return pl.pallas_call(
         finish_kernel,
         out_shape=(shape, shape),
-        in_specs=[hbm, hbm, hbm, hbm],
+        in_specs=[vmem, vmem],
         out_specs=(hbm, hbm),
-        scratch_shapes=[
-            pltpu.VMEM((5,) + load_cases.shape, f32),
-            pltpu.VMEM((1, cases), f32),
-            pltpu.SemaphoreType.DMA((5, rows)),
-            pltpu.SemaphoreType.DMA,
-        ],
-        compiler_params=pltpu.CompilerParams(vmem_limit_bytes=60 * 2**20),
-    )(load_cases, precond, image, alpha)
+        scratch_shapes=[pltpu.SemaphoreType.DMA((2,))],
+        compiler_params=pltpu.CompilerParams(vmem_limit_bytes=32 * 2**20),
+    )(
+        *(pltpu.with_memory_space_constraint(v, pltpu.VMEM) for v in (solved, residual))
+    )
 
 
 def per_device(

time: 37.3 us -> 35.7 us (0.957)
  Pallas kernels: 36.5 us -> 34.9 us
    pallas_call x1, Pallas kernels: 1.88 us -> 0.76 us  [fused(): pl.pallas_call(finish_kernel, out_shape=(shape, shape), in_specs=[vmem, v...]
    pallas_call x1, Pallas kernels: 34.6 us -> 34.1 us  [fused(): pl.pallas_call(functools.partial(step_kernel, nx, ny, modes), out_shape=(...]
where the time goes in v4:
time: 35.7 us; the launch traced here: 35.5 us
  Pallas kernels  34.9 us (98%)
  between operations  0.64 us (2%)
    pallas_call x1, Pallas kernels, fused(): pl.pallas_call(functools.partial(step_kernel, nx, ny, modes), out_shape=(...  34.1 us
    pallas_call x1, Pallas kernels, fused(): pl.pallas_call(finish_kernel, out_shape=(shape, shape), in_specs=[vmem, v...  0.76 us

profile of v4, /device:TPU:0, one launch (start us, length us, event | category | flops | bytes accessed | tf_op | source)
XLA Modules:
  0.0 35.5 jit_solution(3136843601375456956)
XLA Ops:
  0.6 34.1 %shard_map.86 = (f32[2,3,64,128]{3,2,1,0:T(8,128)S(1)}, f32[2,3,64,128]{3,2,1,0:T(8,128)S(1)}) custom-call(f32[2,3,64,128]{3,2,1,0:T(8,128)} %b_hbm.1, f32[2,3,64,320]{3,2,1,0:T(8,128)} %a_hbm.1, s32[3,2,5]{2,1,0:T(2,128)} %bitcast.5, f32[3,2,4096]{2,1,0:T(2,128)} %bitcast.3, f32[3,2,384]{2,1,0:T(2,128)} %bitcast.4, s32[2,3]{1,0:T(2,128)} %map_hbm.1, ...), custom_call_target="tpu_custom_call" | custom-call | tf_op jit(solution)/shard_map/pallas_call | solution.py:509
  34.8 0.8 %shard_map.87 = (f32[2,3,64,128]{3,2,1,0:T(8,128)}, f32[2,3,64,128]{3,2,1,0:T(8,128)}) custom-call(f32[2,3,64,128]{3,2,1,0:T(8,128)S(1)} %get-tuple-element.4.s_ref, f32[2,3,64,128]{3,2,1,0:T(8,128)S(1)} %get-tuple-element.5.r_ref), custom_call_target="tpu_custom_call" | custom-call | tf_op jit(solution)/shard_map/pallas_call | solution.py:571

commit v5 on v4

--- a/solution.py
+++ b/solution.py
@@ -77,9 +77,9 @@
     solution_ref, residual_ref,
     b_ref, a_ref, cols_ref, s_ref, n_ref, map_ref, inv_ref, loaded,
     blocks, nulls, field, up, down, left, right, local, edge, smoother, info, info_all, near, coarse, coarse_all,
-    sums, sums_all, spread, relaxed, relaxed_near, reach, solved,
-    halo_send, halo_recv, near_send, near_recv, relaxed_send, relaxed_recv, col_send, col_recv,
-    all_send, all_recv, direct_send, direct_recv, entered,
+    sums, sums_all, spread, relaxed, relaxed_near, reach, solved, pulls, pulls_near, pushed, pulled,
+    halo_send, halo_recv, near_send, near_recv, relaxed_send, relaxed_recv, pulls_send, pulls_recv, push_send, push_recv, col_send, col_recv,
+    plane_send, plane_recv, pair_send, pair_recv, direct_send, direct_recv, entered,
 ):
     rows, cols, blk, cases = b_ref.shape
     count = rows * cols
@@ -126,6 +126,7 @@
 
     spread[...] = jnp.zeros_like(spread)
     reach[...] = jnp.zeros_like(reach)
+    pulls[...] = jnp.zeros_like(pulls)
     nulls[...] = jnp.zeros_like(nulls)
     info[...] = jnp.zeros_like(info)
     local[...] = jnp.zeros_like(local)
@@ -136,6 +137,8 @@
             halos[side][...] = jnp.zeros_like(halos[side])
             near[side] = jnp.zeros_like(near[side])
             relaxed_near[side] = jnp.zeros_like(relaxed_near[side])
+            pulls_near[side] = jnp.zeros_like(pulls_near[side])
+            pulled[side] = jnp.zeros_like(pulled[side])
 
     told, told_all = info.at[0 : modes + 1], info_all.at[:, 0 : modes + 1]
 
@@ -149,18 +152,35 @@
             for j in range(1, ny)
         ]
 
-    def pass_on(src, dst, slot):
-        for mx in range(nx - 1, 0, -1):
-            pltpu.make_async_remote_copy(
-                src_ref=src, dst_ref=dst.at[slot], send_sem=all_send, recv_sem=all_recv,
-                device_id=(peers_x[mx], y), device_id_type=pl.DeviceIdType.MESH,
-            ).start()
+    def block(mx):
+        return info_all.at[pl.ds(peers_x[mx] * ny, ny), 0 : modes + 1]
+
+    def plane_copy(mx):
+        return pltpu.make_async_remote_copy(
+            src_ref=block(0), dst_ref=block(0), send_sem=plane_send.at[mx // 2],
+            recv_sem=plane_recv.at[mx // 2], device_id=(peers_x[mx], y),
+            device_id_type=pl.DeviceIdType.MESH,
+        )
+
+    def to_sibling(mx):
+        pltpu.make_async_remote_copy(
+            src_ref=block(mx), dst_ref=block(mx), send_sem=pair_send, recv_sem=pair_recv,
+            device_id=(peers_x[1], y), device_id_type=pl.DeviceIdType.MESH,
+        ).start()
+
+    plane = (*range(nx - 2, 0, -2),)
 
     def told_pass():
-        for j in list(range(1, ny, 2)) + list(range(2, ny, 2)):
-            slot = x * ny + lax.rem(y + j, ny)
+        for j in range(1, ny):
             pltpu.make_async_copy(told, told, col_recv.at[j]).wait()
-            pass_on(told_all.at[slot], told_all, slot)
+        for mx in plane:
+            plane_copy(mx).start()
+        to_sibling(0)
+
+    def told_share():
+        for mx in plane[::-1]:
+            pltpu.make_async_copy(block(mx), block(mx), plane_recv.at[mx // 2]).wait()
+            to_sibling(mx)
 
     def wait_many(dst, tiles, sem):
         some = dst.at[pl.ds(0, tiles)]
@@ -199,10 +219,10 @@
         buf = halos[side].at[k]
         pl.when(sides[side][0])(pltpu.make_async_copy(buf, buf, halo_recv.at[k, side]).wait)
 
-    def to_sides(src, dst, send, recv):
+    def to_sides(src, dst, send, recv, split=False):
         return [
             pltpu.make_async_remote_copy(
-                src_ref=src, dst_ref=dst.at[lands],
+                src_ref=src.at[side] if split else src, dst_ref=dst.at[lands],
                 send_sem=send.at[side], recv_sem=recv.at[lands],
                 device_id=peer, device_id_type=pl.DeviceIdType.MESH,
             )
@@ -214,6 +234,12 @@
 
     def relaxed_copies():
         return to_sides(relaxed, relaxed_near, relaxed_send, relaxed_recv)
+
+    def pulls_copies():
+        return to_sides(pulls, pulls_near, pulls_send, pulls_recv, split=True)
+
+    def push_copies():
+        return to_sides(pushed, pulled, push_send, push_recv, split=True)
 
     def from_sides(dst, recv):
         for side, (here, _) in enumerate(sides):
@@ -270,7 +296,6 @@
         pl.semaphore_signal(
             entered, inc=1, device_id=(peers_x[mx], y), device_id_type=pl.DeviceIdType.MESH
         )
-    pass_on(told, told_all, me)
     info_all[pl.ds(me, 1)] = info[...][None]
 
     loads[5].wait()
@@ -326,8 +351,7 @@
     def theirs_all(k):
         return coarse_all.at[k, :, 0:modes]
 
-    def restrict(v, k):
-        g = mm(own_cat, stacked(v))
+    def publish(g, k):
         coarse[k] = g
         to_all(mine(k), theirs_all(k), k)
         coarse_all[k, pl.ds(me, 1)] = g[None]
@@ -361,13 +385,6 @@
         pl.when(here)(copy.start)
     told_pass()
 
-    r = b - operate(first, 0)
-    pl.semaphore_wait(entered, nx - 1)
-    restrict(r, 0)
-    t = smooth(r)
-    put(t, 1)
-    halo_start(1)
-
     reach[0:around] = spread[...] - mm_t(across(relaxed[...]), local[...])
     eye = (
         lax.broadcasted_iota(jnp.int32, (size, size), 0)
@@ -380,7 +397,30 @@
     gain = turned(
         jnp.concatenate([own_n - relaxed[0:8], 0.0 - relaxed[8:around]], axis=0)
     )
-    wait_many(told_all, (nx - 1) * ny, all_recv)
+    for side, at, e, p in places():
+        q = facing[side](at)
+        hi, lo = own_hi[:, p * blk : (p + 1) * blk], own_lo[:, p * blk : (p + 1) * blk]
+        tile, rest = edge[e, :, 0:blk], edge[e, :, 2 * blk : 3 * blk]
+        pulls[side, :, q * blk : (q + 1) * blk] = mm(hi, tile) + (mm(hi, rest) + mm(lo, tile))
+    for (here, _), copy in zip(sides, pulls_copies()):
+        pl.when(here)(copy.start)
+
+    r = b - operate(first, 0)
+    pl.semaphore_wait(entered, nx - 1)
+    publish(mm(own_cat, stacked(r)), 0)
+    t = smooth(r)
+    put(t, 1)
+    halo_start(1)
+    told_share()
+
+    from_sides(relaxed_near, relaxed_recv)
+    for side, at, e, p in places():
+        q = facing[side](at)
+        reach[around * (1 + side) : around * (2 + side), p * blk : (p + 1) * blk] = 0.0 - mm_t(
+            across(relaxed_near[side, :, q * blk : (q + 1) * blk]), edge[e]
+        )
+    reach_turned = turned(reach[...])
+    wait_many(told_all, nx // 2 * ny, pair_recv)
     inv_parts = cut(info_all[...].reshape(coarse_rows, width))
     lane3 = lax.broadcasted_iota(jnp.int32, (n, 8, width), 2).astype(jnp.float32)
     row3 = lax.broadcasted_iota(jnp.int32, (n, 8, width), 1)
@@ -421,23 +461,33 @@
 
     gain_cut = cut(mm3_cut(gain, tuple(part[0:around] for part in solve)))
 
-    from_sides(relaxed_near, relaxed_recv)
-    for side, at, e, p in places():
-        q = facing[side](at)
-        reach[around * (1 + side) : around * (2 + side), p * blk : (p + 1) * blk] = 0.0 - mm_t(
-            across(relaxed_near[side, :, q * blk : (q + 1) * blk]), edge[e]
-        )
-    loss_cut = cut(mm3_cut(turned(reach[...]), solve))
+    loss_cut = cut(mm3_cut(reach_turned, solve))
+
+    from_sides(pulls_near, pulls_recv)
+    inner_pull = mm(own_hi, local[:, 0:size]) + (
+        mm(own_hi, local[:, 2 * size : 3 * size]) + mm(own_lo, local[:, 0:size])
+    )
+    pull_hi, pull_lo = cut(
+        jnp.concatenate([pulls_near[...].reshape(32, size), inner_pull], axis=0)
+    )
+    pull_cat = jnp.concatenate([pull_hi, pull_hi, pull_lo], axis=1)
 
     q1 = r - operate(t, 1)
     g = gathered(0)
     r = q1 - mm3(loss_cut, g)
     s = smooth(r)
+    products = mm(pull_cat, stacked(s))
+    for side in range(4):
+        pushed[side] = products[8 * side : 8 * side + 8]
+    for (here, _), copy in zip(sides, push_copies()):
+        pl.when(here)(copy.start)
     put(s, 2)
     halo_start(2)
+    mine_now = mm(own_cat, stacked(r)) - products[32:40]
     precond = first + t + mm3(gain_cut, g) + s
+    from_sides(pulled, push_recv)
+    publish(mine_now - ((pulled[0] + pulled[1]) + (pulled[2] + pulled[3])), 1)
     r = r - operate(s, 2)
-    restrict(r, 1)
     t = smooth(r)
     put(t, 3)
     halo_start(3)
@@ -463,11 +513,14 @@
             pl.when(here)(copy.wait_send)
     for (here, _), copy in zip(sides, near_copies()):
         pl.when(here)(copy.wait_send)
-    for (here, _), copy in zip(sides, relaxed_copies()):
-        pl.when(here)(copy.wait_send)
+    for copies in (relaxed_copies(), pulls_copies(), push_copies()):
+        for (here, _), copy in zip(sides, copies):
+            pl.when(here)(copy.wait_send)
     for copy in at_column(told, told_all):
         copy.wait_send()
-    wait_many(told_all, (nx - 1) * ny, all_send)
+    for mx in plane:
+        plane_copy(mx).wait_send()
+    wait_many(told_all, nx // 2 * ny, pair_send)
     for k in range(2):
         wait_many(theirs_all(k), n - 1, direct_send.at[k])
     wait_many(pairs, n - 1, direct_recv.at[2])
@@ -542,14 +595,24 @@
             pltpu.VMEM((4, 40, count * blk), f32),
             pltpu.VMEM((256, count * blk), f32),
             pltpu.VMEM((2, n * 8, n * 8), f32),
+            pltpu.VMEM((4, 8, count * blk), f32),
+            pltpu.VMEM((4, 8, count * blk), f32),
+            pltpu.VMEM((4, 8, cases), f32),
+            pltpu.VMEM((4, 8, cases), f32),
             pltpu.SemaphoreType.DMA((4, 4)),
             pltpu.SemaphoreType.DMA((4, 4)),
             pltpu.SemaphoreType.DMA((4,)),
             pltpu.SemaphoreType.DMA((4,)),
             pltpu.SemaphoreType.DMA((4,)),
             pltpu.SemaphoreType.DMA((4,)),
+            pltpu.SemaphoreType.DMA((4,)),
+            pltpu.SemaphoreType.DMA((4,)),
+            pltpu.SemaphoreType.DMA((4,)),
+            pltpu.SemaphoreType.DMA((4,)),
             pltpu.SemaphoreType.DMA((ny,)),
             pltpu.SemaphoreType.DMA((ny,)),
+            pltpu.SemaphoreType.DMA((nx // 2,)),
+            pltpu.SemaphoreType.DMA((nx // 2,)),
             pltpu.SemaphoreType.DMA,
             pltpu.SemaphoreType.DMA,
             pltpu.SemaphoreType.DMA((3,)),

time: 35.7 us -> 34.7 us (0.972)
  Pallas kernels: 34.9 us -> 33.9 us
    pallas_call x1, Pallas kernels: 34.1 us -> 33.1 us  [fused(): pl.pallas_call(functools.partial(step_kernel, nx, ny, modes), out_shape=(...]
where the time goes in v5:
time: 34.7 us; the launch traced here: 34.5 us
  Pallas kernels  33.9 us (98%)
  between operations  0.64 us (2%)
    pallas_call x1, Pallas kernels, fused(): pl.pallas_call(functools.partial(step_kernel, nx, ny, modes), out_shape=(...  33.1 us
    pallas_call x1, Pallas kernels, fused(): pl.pallas_call(finish_kernel, out_shape=(shape, shape), in_specs=[vmem, v...  0.76 us

profile of v5, /device:TPU:0, one launch (start us, length us, event | category | flops | bytes accessed | tf_op | source)
XLA Modules:
  0.0 34.5 jit_solution(2712326872690593609)
XLA Ops:
  0.6 33.1 %shard_map.86 = (f32[2,3,64,128]{3,2,1,0:T(8,128)S(1)}, f32[2,3,64,128]{3,2,1,0:T(8,128)S(1)}) custom-call(f32[2,3,64,128]{3,2,1,0:T(8,128)} %b_hbm.1, f32[2,3,64,320]{3,2,1,0:T(8,128)} %a_hbm.1, s32[3,2,5]{2,1,0:T(2,128)} %bitcast.5, f32[3,2,4096]{2,1,0:T(2,128)} %bitcast.3, f32[3,2,384]{2,1,0:T(2,128)} %bitcast.4, s32[2,3]{1,0:T(2,128)} %map_hbm.1, ...), custom_call_target="tpu_custom_call" | custom-call | tf_op jit(solution)/shard_map/pallas_call | solution.py:562
  33.8 0.8 %shard_map.87 = (f32[2,3,64,128]{3,2,1,0:T(8,128)}, f32[2,3,64,128]{3,2,1,0:T(8,128)}) custom-call(f32[2,3,64,128]{3,2,1,0:T(8,128)S(1)} %get-tuple-element.4.s_ref, f32[2,3,64,128]{3,2,1,0:T(8,128)S(1)} %get-tuple-element.5.r_ref), custom_call_target="tpu_custom_call" | custom-call | tf_op jit(solution)/shard_map/pallas_call | solution.py:634

commit v6 on v5

--- a/solution.py
+++ b/solution.py
@@ -331,8 +331,13 @@
         for i in range(rows):
             yield 3, i, 2 * cols + rows + i, i * cols + cols - 1
 
+    def own_part(v):
+        return mm(local[...], stacked(v))
+
     def operate(v, k):
-        inner = mm(local[...], stacked(v))
+        return beyond(own_part(v), k)
+
+    def beyond(inner, k):
         parts = [inner[p * blk : (p + 1) * blk] for p in range(count)]
         for side in (2, 3, 0, 1):
             halo_wait(k, side)
@@ -492,14 +497,14 @@
     put(t, 3)
     halo_start(3)
     precond = precond + t
-    q2 = r - operate(t, 3)
-    base = b - q2
+    inner = (b - r) + own_part(t)
     g = gathered(1)
     precond = precond + mm3(gain_cut, g)
-    image = base + mm3(loss_cut, g)
+    aligned = jnp.sum(b * precond, axis=0, keepdims=True)
+    image = beyond(inner + mm3(loss_cut, g), 3)
     sums[...] = jnp.concatenate(
         [
-            jnp.sum(b * precond, axis=0, keepdims=True),
+            aligned,
             jnp.sum(precond * image, axis=0, keepdims=True),
             jnp.zeros((6, cases), jnp.float32),
         ],

time: 34.7 us -> 34.2 us (0.986)
  Pallas kernels: 33.9 us -> 33.4 us
    pallas_call x1, Pallas kernels: 33.1 us -> 32.7 us  [fused(): pl.pallas_call(functools.partial(step_kernel, nx, ny, modes), out_shape=(...]
where the time goes in v6:
time: 34.2 us; the launch traced here: 34.1 us
  Pallas kernels  33.4 us (98%)
  between operations  0.64 us (2%)
    pallas_call x1, Pallas kernels, fused(): pl.pallas_call(functools.partial(step_kernel, nx, ny, modes), out_shape=(...  32.7 us
    pallas_call x1, Pallas kernels, fused(): pl.pallas_call(finish_kernel, out_shape=(shape, shape), in_specs=[vmem, v...  0.76 us

profile of v6, /device:TPU:0, one launch (start us, length us, event | category | flops | bytes accessed | tf_op | source)
XLA Modules:
  0.0 34.1 jit_solution(8857790152803490233)
XLA Ops:
  0.6 32.7 %shard_map.86 = (f32[2,3,64,128]{3,2,1,0:T(8,128)S(1)}, f32[2,3,64,128]{3,2,1,0:T(8,128)S(1)}) custom-call(f32[2,3,64,128]{3,2,1,0:T(8,128)} %b_hbm.1, f32[2,3,64,320]{3,2,1,0:T(8,128)} %a_hbm.1, s32[3,2,5]{2,1,0:T(2,128)} %bitcast.5, f32[3,2,4096]{2,1,0:T(2,128)} %bitcast.3, f32[3,2,384]{2,1,0:T(2,128)} %bitcast.4, s32[2,3]{1,0:T(2,128)} %map_hbm.1, ...), custom_call_target="tpu_custom_call" | custom-call | tf_op jit(solution)/shard_map/pallas_call | solution.py:567
  33.3 0.8 %shard_map.87 = (f32[2,3,64,128]{3,2,1,0:T(8,128)}, f32[2,3,64,128]{3,2,1,0:T(8,128)}) custom-call(f32[2,3,64,128]{3,2,1,0:T(8,128)S(1)} %get-tuple-element.4.s_ref, f32[2,3,64,128]{3,2,1,0:T(8,128)S(1)} %get-tuple-element.5.r_ref), custom_call_target="tpu_custom_call" | custom-call | tf_op jit(solution)/shard_map/pallas_call | solution.py:639

commit v7 on v6

--- a/solution.py
+++ b/solution.py
@@ -111,19 +111,21 @@
             )
         )
     ]
-    for load in loads:
+    for load in loads[0:2]:
         load.start()
 
     coarse_all[...] = jnp.zeros_like(coarse_all)
     info_all[...] = jnp.zeros_like(info_all)
 
     lines = [pair for pair in order_of_peers if 0 in pair]
-    for mx, my in lines:
+    for mx, my in lines[::-1]:
         pl.semaphore_signal(
             barrier, inc=1, device_id=(peers_x[mx], peers_y[my]),
             device_id_type=pl.DeviceIdType.MESH,
         )
 
+    for load in loads[2:]:
+        load.start()
     spread[...] = jnp.zeros_like(spread)
     reach[...] = jnp.zeros_like(reach)
     pulls[...] = jnp.zeros_like(pulls)
@@ -347,6 +349,7 @@
         return jnp.concatenate(parts, axis=0)
 
     own_n = nulls[...]
+    inner_first = own_part(first)
     own_hi, own_lo = cut(own_n)
     own_cat = jnp.concatenate([own_hi, own_hi, own_lo], axis=1)
 
@@ -410,7 +413,11 @@
     for (here, _), copy in zip(sides, pulls_copies()):
         pl.when(here)(copy.start)
 
-    r = b - operate(first, 0)
+    inner_pull = mm(own_hi, local[:, 0:size]) + (
+        mm(own_hi, local[:, 2 * size : 3 * size]) + mm(own_lo, local[:, 0:size])
+    )
+
+    r = b - beyond(inner_first, 0)
     pl.semaphore_wait(entered, nx - 1)
     publish(mm(own_cat, stacked(r)), 0)
     t = smooth(r)
@@ -461,17 +468,18 @@
         for k in range(2)
     )
 
+    def laid(v):
+        hi, lo = cut(v)
+        return jnp.concatenate([hi, hi, lo], axis=1)
+
     def mm3_cut(a_cut, b_cut):
         return mm(a_cut[0], b_cut[0]) + (mm(a_cut[0], b_cut[1]) + mm(a_cut[1], b_cut[0]))
 
-    gain_cut = cut(mm3_cut(gain, tuple(part[0:around] for part in solve)))
-
-    loss_cut = cut(mm3_cut(reach_turned, solve))
+    gain_laid = laid(mm3_cut(gain, tuple(part[0:around] for part in solve)))
+
+    loss_laid = laid(mm3_cut(reach_turned, solve))
 
     from_sides(pulls_near, pulls_recv)
-    inner_pull = mm(own_hi, local[:, 0:size]) + (
-        mm(own_hi, local[:, 2 * size : 3 * size]) + mm(own_lo, local[:, 0:size])
-    )
     pull_hi, pull_lo = cut(
         jnp.concatenate([pulls_near[...].reshape(32, size), inner_pull], axis=0)
     )
@@ -479,7 +487,7 @@
 
     q1 = r - operate(t, 1)
     g = gathered(0)
-    r = q1 - mm3(loss_cut, g)
+    r = q1 - mm(loss_laid, stacked(g))
     s = smooth(r)
     products = mm(pull_cat, stacked(s))
     for side in range(4):
@@ -489,7 +497,7 @@
     put(s, 2)
     halo_start(2)
     mine_now = mm(own_cat, stacked(r)) - products[32:40]
-    precond = first + t + mm3(gain_cut, g) + s
+    precond = first + t + mm(gain_laid, stacked(g)) + s
     from_sides(pulled, push_recv)
     publish(mine_now - ((pulled[0] + pulled[1]) + (pulled[2] + pulled[3])), 1)
     r = r - operate(s, 2)
@@ -499,9 +507,9 @@
     precond = precond + t
     inner = (b - r) + own_part(t)
     g = gathered(1)
-    precond = precond + mm3(gain_cut, g)
+    precond = precond + mm(gain_laid, stacked(g))
     aligned = jnp.sum(b * precond, axis=0, keepdims=True)
-    image = beyond(inner + mm3(loss_cut, g), 3)
+    image = beyond(inner + mm(loss_laid, stacked(g)), 3)
     sums[...] = jnp.concatenate(
         [
             aligned,

time: 34.2 us -> 34.2 us (level)
  no operation moved by 1% of the time
where the time goes in v7:
time: 34.2 us; the launch traced here: 34 us
  Pallas kernels  33.4 us (98%)
  between operations  0.64 us (2%)
    pallas_call x1, Pallas kernels, fused(): pl.pallas_call(functools.partial(step_kernel, nx, ny, modes), out_shape=(...  32.6 us
    pallas_call x1, Pallas kernels, fused(): pl.pallas_call(finish_kernel, out_shape=(shape, shape), in_specs=[vmem, v...  0.76 us

profile of v7, /device:TPU:0, one launch (start us, length us, event | category | flops | bytes accessed | tf_op | source)
XLA Modules:
  0.0 34.0 jit_solution(3043343732090951164)
XLA Ops:
  0.6 32.6 %shard_map.86 = (f32[2,3,64,128]{3,2,1,0:T(8,128)S(1)}, f32[2,3,64,128]{3,2,1,0:T(8,128)S(1)}) custom-call(f32[2,3,64,128]{3,2,1,0:T(8,128)} %b_hbm.1, f32[2,3,64,320]{3,2,1,0:T(8,128)} %a_hbm.1, s32[3,2,5]{2,1,0:T(2,128)} %bitcast.5, f32[3,2,4096]{2,1,0:T(2,128)} %bitcast.3, f32[3,2,384]{2,1,0:T(2,128)} %bitcast.4, s32[2,3]{1,0:T(2,128)} %map_hbm.1, ...), custom_call_target="tpu_custom_call" | custom-call | tf_op jit(solution)/shard_map/pallas_call | solution.py:575
  33.3 0.8 %shard_map.87 = (f32[2,3,64,128]{3,2,1,0:T(8,128)}, f32[2,3,64,128]{3,2,1,0:T(8,128)}) custom-call(f32[2,3,64,128]{3,2,1,0:T(8,128)S(1)} %get-tuple-element.4.s_ref, f32[2,3,64,128]{3,2,1,0:T(8,128)S(1)} %get-tuple-element.5.r_ref), custom_call_target="tpu_custom_call" | custom-call | tf_op jit(solution)/shard_map/pallas_call | solution.py:647
